TPU v7x, 32 devices: a whole 2x2x4 slice. The times are simulated.
32 devices in a mesh: lon: 8 (over z, x), lat: 4 (over y, core).
Axes of the slice: x: 2, y: 2, z: 4, core: 2. Of those that a mesh axis runs over, the one named last changes fastest.
Arguments:
- kappa_east: float32 [64, 1024], P('lat', 'lon'), may hold values from 0.02 to 0.2
- kappa_north: float32 [64, 1024], P('lat', 'lon'), may hold values from 0.02 to 0.2
- depth: int32 [64, 1024], P('lat', 'lon'), may hold values from 0 to 75
- sigma: float32 [151], replicated, may hold values from 0.3 to 3
- obs_precision: float32 [151], replicated, may hold values from 0.5 to 4
- obs_tile: int32 [4096, 1], P(('lon', 'lat')), may hold values from 0 to 7; in each aligned block of 128 rows (0 to 127, 128 to 255, ...) at most 32 rows name the same one
- obs_col: int32 [4096], P(('lon', 'lat')), may hold values from 0 to 127
- obs_lat: int32 [4096], P(('lon', 'lat')), may hold values from 0 to 15
- innovation: float32 [151, 4096], P(None, ('lon', 'lat')), may hold values from -6 to 6
Outputs:
- increment: float32 [151, 64, 1024], P(None, 'lat', 'lon')
- residual: float32 [151, 64, 1024], P(None, 'lat', 'lon')
Inputs may be any that keep to these rules, and one draw needn't show every extreme that they name: `obs_tile`: among the 128 profiles listed on one device, no longitude tile is named by more than 32, a bound that some block reaches.
All inputs are finite; a program needn't handle non-finite values.
Results may differ from a plain program's by a relative error of at most 0.00013.
Values sent between devices are 32-bit elements; how exact they have to be, the bound alone decides.
A program may use at most 128 MiB of HBM per device.

v0:
```python
import jax
import jax.numpy as jnp
from jax import lax
from jax.sharding import PartitionSpec as P

NZ = 75
ITERS = 2


def padded(cells, sides, width):
    for axis, dim in sides:
        count = lax.axis_size(axis)
        head = lax.slice_in_dim(cells, 0, width, axis=dim)
        tail = lax.slice_in_dim(cells, cells.shape[dim] - width, cells.shape[dim], axis=dim)
        cells = jnp.concatenate(
            [
                lax.ppermute(tail, axis, [(i, (i + 1) % count) for i in range(count)]),
                cells,
                lax.ppermute(head, axis, [((i + 1) % count, i) for i in range(count)]),
            ],
            axis=dim,
        )
    return cells


def pass_step(v, face_east, face_north):
    centre = v[:, 1:-1, 1:-1]
    out = centre + face_east[:, 1:-1, 1:-1] * (v[:, 1:-1, 2:] - centre)
    out = out + face_east[:, 1:-1, :-2] * (v[:, 1:-1, :-2] - centre)
    out = out + face_north[:, 1:-1, 1:-1] * (v[:, 2:, 1:-1] - centre)
    return out + face_north[:, :-2, 1:-1] * (v[:, :-2, 1:-1] - centre)


def smooth_five(v, face_east, face_north):
    east_one = face_east[:, 4:-4, 4:-4]
    north_one = face_north[:, 4:-4, 4:-4]
    for step in range(5):
        wide = padded(v, (("lon", 2), ("lat", 1)), 1)
        v = pass_step(wide, east_one, north_one)
    return v


def local(
    kappa_east, kappa_north, depth, sigma, obs_precision, obs_tile, obs_col, obs_lat, innovation
):
    rows, cols = kappa_east.shape
    channels = sigma.shape[0]
    lat_tiles = lax.axis_size("lat")
    lon_tiles = lax.axis_size("lon")
    lat_here = lax.axis_index("lat")
    row_ids = lax.broadcasted_iota(jnp.int32, (rows, cols), 0)
    wall = jnp.logical_and(lat_here == lat_tiles - 1, row_ids == rows - 1)
    north_kept = jnp.where(wall, jnp.float32(0.0), kappa_north)
    stacked = jnp.stack([kappa_east, north_kept, depth.astype(jnp.float32)])
    extended = padded(stacked, (("lon", 2), ("lat", 1)), 6)
    levels = jnp.arange(channels, dtype=jnp.int32)
    level_of = jnp.where(levels < 2 * NZ, levels % NZ, 0).astype(jnp.float32)
    wet_ext = (extended[2][None, :, :] > level_of[:, None, None]).astype(jnp.float32)
    face_east = extended[0][None, 1:-1, 1:-1] * wet_ext[:, 1:-1, 1:-1] * wet_ext[:, 1:-1, 2:]
    face_north = extended[1][None, 1:-1, 1:-1] * wet_ext[:, 1:-1, 1:-1] * wet_ext[:, 2:, 1:-1]
    wet_tile = wet_ext[:, 6:-6, 6:-6]
    scale = sigma[:, None, None]
    weight = obs_precision[:, None]
    listed = obs_col.shape[0]
    tile_of = obs_tile[:, 0]
    capacity = max(2, 2 * listed // lon_tiles)
    onehot = (tile_of[:, None] == jnp.arange(lon_tiles, dtype=jnp.int32)[None, :]).astype(jnp.int32)
    before = jnp.cumsum(onehot, axis=0) - onehot
    own_rank = jnp.sum(before * onehot, axis=1)
    slot = tile_of * capacity + own_rank
    local_cell = obs_lat * cols + obs_col
    send_cells = jnp.full((lon_tiles * capacity,), -1, jnp.int32).at[slot].set(local_cell)
    recv_cells = lax.all_to_all(send_cells, "lon", split_axis=0, concat_axis=0, tiled=True)
    valid = (recv_cells >= 0).astype(jnp.float32)
    safe_cells = jnp.maximum(recv_cells, 0)

    def adjoint_obs(w):
        buffer = jnp.zeros((channels, lon_tiles * capacity), jnp.float32).at[:, slot].set(w)
        arrived = lax.all_to_all(buffer, "lon", split_axis=1, concat_axis=1, tiled=True)
        cells = (
            jnp.zeros((channels, rows * cols), jnp.float32)
            .at[:, safe_cells]
            .add(arrived * valid[None, :])
        )
        return cells.reshape(channels, rows, cols) * wet_tile

    def squares(v):
        return lax.psum(jnp.sum(v * v), ("lon", "lat"))

    rhs = smooth_five(scale * adjoint_obs(weight * innovation), face_east, face_north)
    increment = jnp.zeros_like(rhs)
    residual = rhs
    direction = rhs
    norm_now = squares(residual)
    for step in range(ITERS):
        hessian_u = scale * smooth_five(direction, face_east, face_north)
        flat = (hessian_u * wet_tile).reshape(channels, rows * cols)
        picked = jnp.take(flat, safe_cells, axis=1) * valid[None, :]
        back = lax.all_to_all(picked, "lon", split_axis=1, concat_axis=1, tiled=True)
        hessian_w = weight * jnp.take(back, slot, axis=1)
        image = direction + smooth_five(scale * adjoint_obs(hessian_w), face_east, face_north)
        alpha = norm_now / lax.psum(jnp.sum(direction * image), ("lon", "lat"))
        increment = increment + alpha * direction
        residual = residual - alpha * image
        norm_next = squares(residual)
        direction = residual + norm_next / norm_now * direction
        norm_now = norm_next
    return (increment, residual)


def solution(mesh):
    return jax.shard_map(
        local,
        mesh=mesh,
        in_specs=(
            P("lat", "lon"),
            P("lat", "lon"),
            P("lat", "lon"),
            P(),
            P(),
            P(("lon", "lat"), None),
            P(("lon", "lat")),
            P(("lon", "lat")),
            P(None, ("lon", "lat")),
        ),
        out_specs=(P(None, "lat", "lon"), P(None, "lat", "lon")),
        check_vma=False,
    )
```

profile of v0, /device:TPU:0, one launch (start us, length us, event | category | flops | bytes accessed | tf_op | source)
XLA Modules:
  0.0 661.0 jit_solution(5693233168611691165)
XLA Ops:
  23.4 5.0 all-to-all-start.1
  32.2 5.3 all-to-all-done.1
  53.6 7.9 %slice_multiply_fusion.1 = (f32[151,26,138]{0,1,2:T(8,128)S(1)}, f32[151,26,138]{0,1,2:T(8,128)S(1)}) fusion(f32[151,28,140]{0,1,2:T(8,128)} %compare_convert_fusion, f32[26,138]{0,1:T(8,128)S(1)} %copy.27, f32[26,138]{0,1:T(8,128)S(1)} %copy.28), kind=kLoop, calls=%fused_computation.13 | loop fusion | flops 2167152 | bytes 10864464 | tf_op jit(solution)/shard_map/mul | solution.py:59
  78.9 4.8 collective-permute-start.12
  93.6 4.8 collective-permute-start.16
  139.1 4.8 collective-permute-start.28
  154.7 4.8 collective-permute-start.32
  170.3 4.8 collective-permute-start.36
  185.7 4.8 collective-permute-start.40
  208.7 6.1 all-to-all-start.2
  214.8 8.5 %all-to-all-done.2 = f32[151,8,32]{0,2,1:T(8,128)S(1)} async-done(((f32[151,8,32]{0,2,1:T(8,128)}), f32[151,8,32]{0,2,1:T(8,128)S(1)}, u32[]{:S(2)}, u32[]{:S(2)}) %all-to-all-start.2) | async-done | bytes 154656 | tf_op jit(solution)/shard_map/all_to_all | solution.py:99
  224.7 11.9 %all_to_all.69 = f32[151,8,32]{0,2,1:T(8,128)S(1)} all-to-all(f32[151,8,32]{0,2,1:T(8,128)S(1)} %bitcast.94), channel_id=1, replica_groups=mesh['lon'=8,'lat'=4] {'lon'}, dimensions={1} | all-to-all | bytes 309248 | tf_op jit(solution)/shard_map/all_to_all | solution.py:79
  320.5 41.2 %all-reduce = (f32[]{:T(128)}, f32[]{:T(128)}) all-reduce(f32[]{:T(128)} %get-tuple-element.7, f32[]{:T(128)} %get-tuple-element.6), channel_id=1, replica_groups=mesh['lon'=8,'lat'=4] {'lon','lat'}, use_global_device_ids=true, to_apply=%region_6.7 | all-reduce | flops 2 | bytes 16 | tf_op jit(solution)/shard_map/psum | solution.py:88
  365.8 40.6 %psum.30 = f32[]{:T(128)} all-reduce(f32[]{:T(128)} %multiply_reduce_fusion.1), channel_id=1, replica_groups=mesh['lon'=8,'lat'=4] {'lon','lat'}, use_global_device_ids=true, to_apply=%region_12.15 | all-reduce | flops 1 | bytes 8 | tf_op jit(solution)/shard_map/psum | solution.py:88
  442.8 4.8 collective-permute-start.72
  457.6 4.8 collective-permute-start.76
  473.0 4.8 collective-permute-start.80
  494.8 14.5 %all_to_all.70 = f32[151,8,32]{0,2,1:T(8,128)S(1)} all-to-all(f32[151,8,32]{0,2,1:T(8,128)S(1)} %bitcast.93), channel_id=1, replica_groups=mesh['lon'=8,'lat'=4] {'lon'}, dimensions={1} | all-to-all | bytes 309248 | tf_op jit(solution)/shard_map/all_to_all | solution.py:99
  510.7 14.0 %all_to_all.71 = f32[151,8,32]{0,2,1:T(8,128)S(1)} all-to-all(f32[151,8,32]{0,2,1:T(8,128)S(1)} %bitcast.92), channel_id=1, replica_groups=mesh['lon'=8,'lat'=4] {'lon'}, dimensions={1} | all-to-all | bytes 309248 | tf_op jit(solution)/shard_map/all_to_all | solution.py:79
  563.1 4.8 collective-permute-start.92
  577.4 5.0 collective-permute-start.96
  592.2 5.1 collective-permute-start.100
  609.5 39.3 %psum.31 = f32[]{:T(128)} all-reduce(f32[]{:T(128)} %get-tuple-element.10), channel_id=1, replica_groups=mesh['lon'=8,'lat'=4] {'lon','lat'}, use_global_device_ids=true, to_apply=%region_16.19 | all-reduce | flops 1 | bytes 8 | tf_op jit(solution)/shard_map/psum | solution.py:102
  650.1 5.9 multiply_subtract_fusion
  (471 shorter events, 395.4 us)
Async XLA Ops:
  2.9 17.0 %collective-permute-start = (f32[3,16,6]{2,1,0:T(8,128)S(1)}, f32[3,16,6]{2,1,0:T(8,128)S(1)}, u32[]{:S(2)}, u32[]{:S(2)}) collective-permute-start(f32[3,16,6]{2,1,0:T(8,128)S(1)} %get-tuple-element.124), channel_id=1, source_target_pairs={{0,4},{4,8},{8,12},{12,16},{16,20},{20,24},{24,28},{28,0},{1,5},{5... | collective-permute-start | bytes 3464 | tf_op jit(solution)/shard_map/ppermute | solution.py:17
  5.9 14.0 %collective-permute-start.1 = (f32[3,16,6]{2,1,0:T(8,128)S(1)}, f32[3,16,6]{2,1,0:T(8,128)S(1)}, u32[]{:S(2)}, u32[]{:S(2)}) collective-permute-start(f32[3,16,6]{2,1,0:T(8,128)S(1)} %get-tuple-element.125), channel_id=1, source_target_pairs={{4,0},{8,4},{12,8},{16,12},{20,16},{24,20},{28,24},{0,28},{5,1},{9... | collective-permute-start | bytes 3464 | tf_op jit(solution)/shard_map/ppermute | solution.py:19
  13.7 9.7 %all-to-all-start = ((s32[8,32,1]{1,2,0:T(1,128)}), s32[8,32,1]{1,2,0:T(1,128)S(1)}, u32[]{:S(2)}, u32[]{:S(2)}) async-start(s32[8,32,1]{1,2,0:T(1,128)} %bitcast.3), calls=%async_computation | async-start | bytes 8192 | tf_op jit(solution)/shard_map/all_to_all | solution.py:73
  20.7 7.9 %collective-permute-start.2 = (f32[3,6,140]{2,1,0:T(8,128)S(1)}, f32[3,6,140]{2,1,0:T(8,128)S(1)}, u32[]{:S(2)}, u32[]{:S(2)}) collective-permute-start(f32[3,6,140]{2,1,0:T(8,128)S(1)} %get-tuple-element.122), channel_id=1, source_target_pairs={{0,1},{1,2},{2,3},{3,0},{4,5},{5,6},{6,7},{7,4},{8,9},{9,10},{10,1... | collective-permute-start | bytes 30248 | tf_op jit(solution)/shard_map/ppermute | solution.py:17
  20.7 7.9 %collective-permute-start.3 = (f32[3,6,140]{2,1,0:T(8,128)S(1)}, f32[3,6,140]{2,1,0:T(8,128)S(1)}, u32[]{:S(2)}, u32[]{:S(2)}) collective-permute-start(f32[3,6,140]{2,1,0:T(8,128)S(1)} %get-tuple-element.123), channel_id=1, source_target_pairs={{1,0},{2,1},{3,2},{0,3},{5,4},{6,5},{7,6},{4,7},{9,8},{10,9},{11,1... | collective-permute-start | bytes 30248 | tf_op jit(solution)/shard_map/ppermute | solution.py:19
  23.4 14.1 %all-to-all-start.1 = ((f32[151,8,32]{0,2,1:T(8,128)}), f32[151,8,32]{0,2,1:T(8,128)S(1)}, u32[]{:S(2)}, u32[]{:S(2)}) async-start(f32[151,8,32]{0,2,1:T(8,128)} %bitcast.5), calls=%async_computation.1 | async-start | bytes 524288 | tf_op jit(solution)/shard_map/all_to_all | solution.py:79
  51.8 9.8 %collective-permute-start.7 = (f32[151,1,130]{0,2,1:T(8,128)S(1)}, f32[151,1,130]{0,2,1:T(8,128)S(1)}, u32[]{:S(2)}, u32[]{:S(2)}) collective-permute-start(f32[151,1,130]{0,2,1:T(8,128)S(1)} %copy.31), channel_id=1, source_target_pairs={{0,1},{1,2},{2,3},{3,0},{4,5},{5,6},{6,7},{7,4},{8,9},{9,10},{10,1... | collective-permute-start | bytes 235568 | tf_op jit(solution)/shard_map/ppermute | solution.py:17
  51.8 9.9 %collective-permute-start.6 = (f32[151,1,130]{0,2,1:T(8,128)S(1)}, f32[151,1,130]{0,2,1:T(8,128)S(1)}, u32[]{:S(2)}, u32[]{:S(2)}) collective-permute-start(f32[151,1,130]{0,2,1:T(8,128)S(1)} %copy.29), channel_id=1, source_target_pairs={{1,0},{2,1},{3,2},{0,3},{5,4},{6,5},{7,6},{4,7},{9,8},{10,9},{11,1... | collective-permute-start | bytes 235568 | tf_op jit(solution)/shard_map/ppermute | solution.py:19
  78.9 6.6 collective-permute-start.13
  93.5 6.7 %collective-permute-start.17 = (f32[151,16,1]{0,1,2:T(8,128)S(1)}, f32[151,16,1]{0,1,2:T(8,128)S(1)}, u32[]{:S(2)}, u32[]{:S(2)}) collective-permute-start(f32[151,16,1]{0,1,2:T(8,128)S(1)} %get-tuple-element.111), channel_id=1, source_target_pairs={{0,4},{4,8},{8,12},{12,16},{16,20},{20,24},{24,28},{28,0},{1,5},{5... | collective-permute-start | bytes 29000 | tf_op jit(solution)/shard_map/ppermute | solution.py:17
  93.6 6.6 collective-permute-start.16
  139.0 6.5 collective-permute-start.29
  154.6 6.6 collective-permute-start.33
  170.2 6.5 collective-permute-start.37
  185.7 6.6 collective-permute-start.41
  208.7 14.6 %all-to-all-start.2 = ((f32[151,8,32]{0,2,1:T(8,128)}), f32[151,8,32]{0,2,1:T(8,128)S(1)}, u32[]{:S(2)}, u32[]{:S(2)}) async-start(f32[151,8,32]{0,2,1:T(8,128)} %bitcast.17), calls=%async_computation.2 | async-start | bytes 524288 | tf_op jit(solution)/shard_map/all_to_all | solution.py:99
  442.8 6.6 collective-permute-start.73
  457.6 6.6 collective-permute-start.77
  473.0 6.6 collective-permute-start.81
  563.0 6.6 collective-permute-start.93
  577.3 6.7 %collective-permute-start.97 = (f32[151,16,1]{0,1,2:T(8,128)S(1)}, f32[151,16,1]{0,1,2:T(8,128)S(1)}, u32[]{:S(2)}, u32[]{:S(2)}) collective-permute-start(f32[151,16,1]{0,1,2:T(8,128)S(1)} %get-tuple-element.71), channel_id=1, source_target_pairs={{0,4},{4,8},{8,12},{12,16},{16,20},{20,24},{24,28},{28,0},{1,5},{5... | collective-permute-start | bytes 29000 | tf_op jit(solution)/shard_map/ppermute | solution.py:17
  577.4 6.7 %collective-permute-start.96 = (f32[151,16,1]{0,1,2:T(8,128)S(1)}, f32[151,16,1]{0,1,2:T(8,128)S(1)}, u32[]{:S(2)}, u32[]{:S(2)}) collective-permute-start(f32[151,16,1]{0,1,2:T(8,128)S(1)} %get-tuple-element.72), channel_id=1, source_target_pairs={{4,0},{8,4},{12,8},{16,12},{20,16},{24,20},{28,24},{0,28},{5,1},{9... | collective-permute-start | bytes 29000 | tf_op jit(solution)/shard_map/ppermute | solution.py:19
  592.2 6.9 %collective-permute-start.101 = (f32[151,16,1]{0,1,2:T(8,128)S(1)}, f32[151,16,1]{0,1,2:T(8,128)S(1)}, u32[]{:S(2)}, u32[]{:S(2)}) collective-permute-start(f32[151,16,1]{0,1,2:T(8,128)S(1)} %get-tuple-element.69), channel_id=1, source_target_pairs={{0,4},{4,8},{8,12},{12,16},{16,20},{20,24},{24,28},{28,0},{1,5},{5... | collective-permute-start | bytes 29000 | tf_op jit(solution)/shard_map/ppermute | solution.py:17
  592.2 6.8 %collective-permute-start.100 = (f32[151,16,1]{0,1,2:T(8,128)S(1)}, f32[151,16,1]{0,1,2:T(8,128)S(1)}, u32[]{:S(2)}, u32[]{:S(2)}) collective-permute-start(f32[151,16,1]{0,1,2:T(8,128)S(1)} %get-tuple-element.70), channel_id=1, source_target_pairs={{4,0},{8,4},{12,8},{16,12},{20,16},{24,20},{28,24},{0,28},{5,1},{9... | collective-permute-start | bytes 29000 | tf_op jit(solution)/shard_map/ppermute | solution.py:19
  (102 other events, 981.0 us)
where the time goes:
time: 670 us; the launch traced here: 661 us
  starting transfers between devices  191 us (29%)
  blocking collectives  162 us (24%)
  other arithmetic  138 us (21%)
  waiting for transfers between devices  138 us (21%)
  local copies, waits for them, and re-layouts  26 us (4%)
  between operations  6.91 us (1%)
    ppermute x52, starting transfers between devices, padded(): lax.ppermute(head, axis, [((i + 1) % count, i) for i in range(count)])  155 us
    ppermute x52, waiting for transfers between devices, padded(): lax.ppermute(tail, axis, [(i, (i + 1) % count) for i in range(count)])  115 us
    psum x2, blocking collectives, squares(): return lax.psum(jnp.sum(v * v), ('lon', 'lat'))  81.8 us
    add x21, other arithmetic, pass_step(): return out + face_north[:, :-2, 1:-1] * (v[:, :-2, 1:-1] - centre)  57.8 us
    psum x1, blocking collectives, local(): alpha = norm_now / lax.psum(jnp.sum(direction * image), ('lon', 'lat'))  39.3 us
    all_to_all x2, blocking collectives, adjoint_obs(): lax.all_to_all(buffer, 'lon', split_axis=1, concat_axis=1, tiled=True)  25.9 us
    ppermute x52, starting transfers between devices, padded(): lax.ppermute(tail, axis, [(i, (i + 1) % count) for i in range(count)])  21.5 us
    all_to_all x1, blocking collectives, local(): lax.all_to_all(picked, 'lon', split_axis=1, concat_axis=1, tiled=True)  14.5 us
  transfers between devices with their start and end apart: 107, of which 62 were waited for; matrix products, arithmetic and copies ran while one was open for 4% of the time, Pallas kernels for 0%

commit v1 on v0

v1 whole, which is shorter than its diff:
```python
import functools

import jax
import jax.numpy as jnp
from jax import lax
from jax.experimental import pallas as pl
from jax.experimental.pallas import tpu as pltpu
from jax.sharding import PartitionSpec as P

NZ = 75
AXES = ("lon", "lat")


def smooth_kernel(lev, x, ke, kw, kn, de, dw, dn, *rest):
    if len(rest) == 8:
        gain, out, va, vb, fe, fw, fn, dd = rest
    else:
        gain = None
        out, va, vb, fe, fw, fn, dd = rest
    channels, rows, tiles, lanes = x.shape
    block = 8
    blocks = rows // block
    zero = jnp.zeros((tiles, lanes), jnp.float32)
    for c in range(channels):
        va[c, 0] = zero
        vb[c, 0] = zero
        va[c, rows + 1] = zero
        vb[c, rows + 1] = zero
        fn[c, 0] = zero

    def build(i, carry):
        c = i // blocks
        r = (i % blocks) * block
        here = pl.ds(r, block)
        level = lev[c]
        east = jnp.where(de[here] > level, ke[here], 0.0)
        west = jnp.where(dw[here] > level, kw[here], 0.0)
        north = jnp.where(dn[here] > level, kn[here], 0.0)
        fe[c, here] = east
        fw[c, here] = west
        fn[c, pl.ds(r + 1, block)] = north
        south = fn[c, here]
        dd[c, here] = 1.0 - (east + west + north + south)
        cells = x[c, here]
        if gain is not None:
            cells = cells * gain[c, here]
        va[c, pl.ds(r + 1, block)] = cells
        return carry

    lax.fori_loop(0, channels * blocks, build, 0)
    lane = lax.broadcasted_iota(jnp.int32, (block, tiles, lanes), 2)

    def step(src, dst, shift):
        def body(i, carry):
            c = i // blocks
            r = (i % blocks) * block
            here = pl.ds(r, block)
            centre = src[c, pl.ds(r + 1, block)]
            east = pltpu.roll(centre, lanes - 1, 2)
            east = jnp.where(lane == lanes - 1, pltpu.roll(east, tiles - 1, 1), east)
            west = pltpu.roll(centre, 1, 2)
            west = jnp.where(lane == 0, pltpu.roll(west, 1, 1), west)
            new = dd[c, here] * centre + fe[c, here] * east + fw[c, here] * west
            new = new + fn[c, pl.ds(r + 1, block)] * src[c, pl.ds(r + 2, block)]
            new = new + fn[c, here] * src[c, here]
            dst[c, pl.ds(r + shift, block)] = new
            return carry

        lax.fori_loop(0, channels * blocks, body, 0)

    step(va, vb, 1)
    step(vb, va, 1)
    step(va, vb, 1)
    step(vb, va, 1)
    step(va, out, 0)


def smooth_five(x, faces, lev, gain=None):
    channels, rows, tiles, lanes = x.shape
    vmem = pl.BlockSpec(memory_space=pltpu.VMEM)
    operands = [lev, x, *faces] + ([] if gain is None else [gain])
    field = pltpu.VMEM((channels, rows, tiles, lanes), jnp.float32)
    padded = pltpu.VMEM((channels, rows + 2, tiles, lanes), jnp.float32)
    cells = channels * rows * tiles * lanes
    return pl.pallas_call(
        smooth_kernel,
        out_shape=jax.ShapeDtypeStruct(x.shape, jnp.float32),
        in_specs=[pl.BlockSpec(memory_space=pltpu.SMEM)] + [vmem] * (len(operands) - 1),
        out_specs=vmem,
        scratch_shapes=[padded, padded, field, field, padded, field],
        cost_estimate=pl.CostEstimate(
            flops=60 * cells, bytes_accessed=16 * cells, transcendentals=0
        ),
        compiler_params=pltpu.CompilerParams(vmem_limit_bytes=48 * 1024 * 1024),
        name="smooth_five",
    )(*operands)


def local(
    kappa_east, kappa_north, depth, sigma, obs_precision, obs_tile, obs_col, obs_lat, innovation
):
    rows, lanes = kappa_east.shape
    total = sigma.shape[0]
    tiles = lax.axis_size("lon")
    bands = lax.axis_size("lat")
    devices = tiles * bands
    channels = -(-total // devices)
    listed = obs_col.shape[0]
    spare = channels * devices - total

    obs_lon = obs_tile[:, 0] * lanes + obs_col
    packed = jnp.concatenate(
        [
            kappa_east.reshape(-1),
            kappa_north.reshape(-1),
            depth.astype(jnp.float32).reshape(-1),
            obs_lon.astype(jnp.float32),
            obs_lat.astype(jnp.float32),
        ]
    ).reshape(-1, lanes)
    everywhere = lax.all_gather(packed, AXES, axis=0, tiled=False)
    maps = everywhere[:, : 3 * rows].reshape(tiles, bands, 3, rows, lanes)
    maps = maps.transpose(2, 1, 3, 0, 4).reshape(3, bands * rows, tiles, lanes)
    places = everywhere[:, 3 * rows :].reshape(tiles, bands, 2, listed)
    places = places.transpose(2, 1, 0, 3).reshape(2, bands, tiles * listed)

    misfit = jnp.pad(obs_precision[:, None] * innovation, ((0, spare), (0, 0)))
    misfit = lax.all_to_all(
        misfit.reshape(devices, channels, listed), AXES, split_axis=0, concat_axis=0, tiled=True
    )
    misfit = misfit.reshape(tiles, bands, channels, listed).transpose(1, 2, 0, 3)
    misfit = misfit.reshape(bands, channels, tiles * listed)

    me = lax.axis_index("lon") * bands + lax.axis_index("lat")
    first = me * channels
    ids = first + jnp.arange(channels, dtype=jnp.int32)
    lev = jnp.where(ids < 2 * NZ, ids % NZ, 0).astype(jnp.float32)
    scale = lax.dynamic_slice(jnp.pad(sigma, (0, spare)), (first,), (channels,))
    weight = lax.dynamic_slice(jnp.pad(obs_precision, (0, spare)), (first,), (channels,))

    height = bands * rows
    ke, kn, deep = maps[0], maps[1], maps[2]

    def shifted(field, by):
        flat = field.reshape(height, tiles * lanes)
        return jnp.roll(flat, by, 1).reshape(field.shape)

    kept = (jnp.arange(height) < height - 1)[:, None, None]
    kn = jnp.where(kept, kn, 0.0)
    de = jnp.minimum(deep, shifted(deep, -1))
    faces = (
        ke,
        shifted(ke, 1),
        kn,
        de,
        shifted(de, 1),
        jnp.minimum(deep, jnp.roll(deep, -1, 0)),
    )

    values = jnp.concatenate([misfit, jnp.ones_like(misfit[:, :1])], axis=1)
    high = lax.reduce_precision(values, 8, 7)
    left = values - high
    middle = lax.reduce_precision(left, 8, 7)
    low = left - middle
    parts = jnp.stack([high, middle, low], axis=1).astype(jnp.bfloat16)
    at_row = places[1][:, None, :] == jnp.arange(rows, dtype=jnp.float32)[None, :, None]
    at_col = (
        places[0][:, None, :] == jnp.arange(tiles * lanes, dtype=jnp.float32)[None, :, None]
    )
    spread = jnp.where(at_row[:, None, None], parts[:, :, :, None, :], 0)
    spread = spread.reshape(bands, 3 * (channels + 1) * rows, tiles * listed)
    cells = lax.dot_general(
        spread,
        at_col.astype(jnp.bfloat16),
        (((2,), (2,)), ((0,), (0,))),
        preferred_element_type=jnp.float32,
    )
    cells = cells.reshape(bands, 3, channels + 1, rows, tiles, lanes).sum(1)
    cells = cells.transpose(1, 0, 2, 3, 4).reshape(channels + 1, height, tiles, lanes)
    wet = (deep[None] > lev[:, None, None, None]).astype(jnp.float32)
    scaled_wet = scale[:, None, None, None] * wet
    gain = scaled_wet * (scale * weight)[:, None, None, None] * cells[channels][None]

    rhs = smooth_five(scaled_wet * cells[:channels], faces, lev)
    q_one = smooth_five(rhs, faces, lev)
    sums = lax.psum(
        jnp.stack([jnp.sum(rhs * rhs), jnp.sum(q_one * q_one * gain)]), AXES
    )
    s_one = smooth_five(q_one, faces, lev, gain)
    norm_zero = sums[0]
    alpha_one = norm_zero / (norm_zero + sums[1])
    r_one = rhs - alpha_one * (rhs + s_one)
    norm_one = lax.psum(jnp.sum(r_one * r_one), AXES)
    t_one = smooth_five(r_one, faces, lev)
    beta = norm_one / norm_zero
    p_two = r_one + beta * rhs
    q_two = t_one + beta * q_one
    curve = lax.psum(jnp.sum(p_two * p_two + q_two * q_two * gain), AXES)
    s_two = smooth_five(q_two, faces, lev, gain)
    alpha_two = norm_one / curve

    def home(field):
        split = field.reshape(channels, bands, rows, tiles, lanes).transpose(3, 1, 0, 2, 4)
        split = split.reshape(devices, channels, rows, lanes)
        moved = lax.all_to_all(split, AXES, split_axis=0, concat_axis=0, tiled=True)
        return moved.reshape(devices * channels, rows, lanes)[:total]

    increment = home(alpha_one * rhs + alpha_two * p_two)
    residual = home(r_one - alpha_two * (p_two + s_two))
    return increment, residual


def solution(mesh):
    return jax.shard_map(
        local,
        mesh=mesh,
        in_specs=(
            P("lat", "lon"),
            P("lat", "lon"),
            P("lat", "lon"),
            P(),
            P(),
            P(("lon", "lat"), None),
            P(("lon", "lat")),
            P(("lon", "lat")),
            P(None, ("lon", "lat")),
        ),
        out_specs=(P(None, "lat", "lon"), P(None, "lat", "lon")),
        check_vma=False,
    )
```

time: 670 us -> 397 us (0.59); the launches traced: 661 us -> 396 us
  starting transfers between devices: 191 us -> 15.4 us
  other arithmetic: 138 us -> 19.8 us
  Pallas kernels: 0 us -> 102 us
  waiting for transfers between devices: 138 us -> 61.2 us
    ppermute x104 -> x0, starting transfers between devices: 177 us -> none  [the longest x52 155 us: padded(): lax.ppermute(head, axis, [((i + 1) % count, i) for i in range(count)])]
    ppermute x104 -> x0, waiting for transfers between devices: 123 us -> none  [the longest x52 115 us: padded(): lax.ppermute(tail, axis, [(i, (i + 1) % count) for i in range(count)])]
    pallas_call x0 -> x5, Pallas kernels: none -> 102 us  [smooth_five(): pl.pallas_call(smooth_kernel, out_shape=jax.ShapeDtypeStruct(x.shape, jnp...]
    add x23 -> x0, other arithmetic: 60.8 us -> none  [the longest x21 57.8 us: pass_step(): return out + face_north[:, :-2, 1:-1] * (v[:, :-2, 1:-1] - centre)]
    all_to_all x3, waiting for transfers between devices: 14.8 us -> 61.2 us  [the longest x2 61.2 us: home(): moved = lax.all_to_all(split, AXES, split_axis=0, concat_axis=0, tiled=True)]
    all_gather x0 -> x1, blocking collectives: none -> 44.3 us  [local(): everywhere = lax.all_gather(packed, AXES, axis=0, tiled=False)]
    all_to_all x3 -> x0, blocking collectives: 40.4 us -> none  [the longest x2 25.9 us: adjoint_obs(): lax.all_to_all(buffer, 'lon', split_axis=1, concat_axis=1, tiled=True)]
    mul x11 -> x3, other arithmetic: 30 us -> 1.28 us  [the longest x1 0.97 us: local(): misfit = jnp.pad(obs_precision[:, None] * innovation, ((0, spare), (0, 0)))]
  transfers between devices with their start and end apart: 107 -> 3, of which waited for: 62 -> 2; matrix products, arithmetic and copies ran while one was open for 4% -> 2% of each run, Pallas kernels for 0% -> 0%
where the time goes in v1:
time: 397 us; the launch traced here: 396 us
  blocking collectives  162 us (41%)
  Pallas kernels  102 us (26%)
  waiting for transfers between devices  61.2 us (15%)
  local copies, waits for them, and re-layouts  26.4 us (7%)
  other arithmetic  19.8 us (5%)
  starting transfers between devices  15.4 us (4%)
  between operations  5.66 us (1%)
    pallas_call x5, Pallas kernels, smooth_five(): pl.pallas_call(smooth_kernel, out_shape=jax.ShapeDtypeStruct(x.shape, jnp...  102 us
    all_to_all x2, waiting for transfers between devices, home(): moved = lax.all_to_all(split, AXES, split_axis=0, concat_axis=0, tiled=True)  61.2 us
    all_gather x1, blocking collectives, local(): everywhere = lax.all_gather(packed, AXES, axis=0, tiled=False)  44.3 us
    psum x1, blocking collectives, local(): norm_one = lax.psum(jnp.sum(r_one * r_one), AXES)  41.5 us
    psum x1, blocking collectives, local(): curve = lax.psum(jnp.sum(p_two * p_two + q_two * q_two * gain), AXES)  39.9 us
    psum x1, blocking collectives, local(): lax.psum(jnp.stack([jnp.sum(rhs * rhs), jnp.sum(q_one * q_one * gain)]),...  36.8 us
    unnamed x59, local copies, waits for them, and re-layouts  16.1 us
    all_to_all x2, starting transfers between devices, home(): moved = lax.all_to_all(split, AXES, split_axis=0, concat_axis=0, tiled=True)  8.05 us
  transfers between devices with their start and end apart: 3, of which 2 were waited for; matrix products, arithmetic and copies ran while one was open for 2% of the time, Pallas kernels for 0%

profile of v1, /device:TPU:0, one launch (start us, length us, event | category | flops | bytes accessed | tf_op | source)
XLA Modules:
  0.0 395.7 jit_solution(7116020678176160589)
XLA Ops:
  2.3 7.3 %all-to-all-start = ((f32[32,5,128]{2,1,0:T(8,128)}), f32[32,5,128]{2,1,0:T(8,128)S(1)}, u32[]{:S(2)}, u32[]{:S(2)}) async-start(f32[32,5,128]{2,1,0:T(8,128)} %reshape.144), calls=%async_computation | async-start | bytes 262144 | tf_op jit(solution)/shard_map/all_to_all | solution.py:128
  13.1 44.3 %all_gather.3 = f32[32,50,128]{2,1,0:T(8,128)S(1)} all-gather(f32[1,50,128]{2,1,0:T(8,128)S(1)} %bitcast.134), channel_id=1, replica_groups=mesh['lon'=8,'lat'=4] {'lon','lat'}, dimensions={0}, use_global_device_ids=true | all-gather | bytes 844800 | tf_op jit(solution)/shard_map/all_gather | solution.py:121
  62.0 2.9 fusion
  64.9 3.3 copy.43
  68.2 4.1 %reduce_sum.45 = f32[4,6,16,8,128]{4,3,2,1,0:T(8,128)} reduce(f32[4,3,6,16,8,128]{5,4,3,2,1,0:T(8,128)} %bitcast.106, f32[]{:T(128)} %constant.37.clone.1), dimensions={1}, to_apply=%region_0.1 | reduce | flops 786432 | bytes 6291460 | tf_op jit(solution)/shard_map/reduce_sum | solution.py:178
  72.2 1.4 slice.105
  75.0 20.4 %smooth_five.5.x = f32[5,64,8,128]{3,2,1,0:T(8,128)S(1)} custom-call(f32[5]{0:T(128)S(1)} %fusion.11.lev, f32[5,64,8,128]{3,2,1,0:T(8,128)S(1)} %select_multiply_fusion.1.x, f32[64,8,128]{2,1,0:T(8,128)S(1)} %bitcast.91, f32[64,8,128]{2,1,0:T(8,128)S(1)} %bitcast.96, f32[64,8,128]{2,1,0:T(8,128)S(1)} %get-tuple-element.26.kn, ...), custom_call_target="tpu_custom_call" | custom-call | flops 19660800 | bytes 5242880 | tf_op jit(solution)/shard_map/smooth_five/pallas_call | solution.py:85
  98.2 20.4 %smooth_five.6.x = f32[5,64,8,128]{3,2,1,0:T(8,128)S(1)} custom-call(f32[5]{0:T(128)S(1)} %fusion.11.lev, f32[5,64,8,128]{3,2,1,0:T(8,128)S(1)} %smooth_five.5.x, f32[64,8,128]{2,1,0:T(8,128)S(1)} %bitcast.92, f32[64,8,128]{2,1,0:T(8,128)S(1)} %bitcast.97, f32[64,8,128]{2,1,0:T(8,128)S(1)} %copy-done.11, f32[64,8,128]{2,1,0:T(8,128)S(1)} %copy-done.8, ...), custom_call_target="tpu_custom_call" | custom-call | flops 19660800 | bytes 5242880 | tf_op jit(solution)/shard_map/smooth_five/pallas_call | solution.py:85
  120.7 1.3 pad_maximum_fusion.2
  122.1 20.4 %smooth_five.7 = f32[5,64,8,128]{3,2,1,0:T(8,128)S(1)} custom-call(f32[5]{0:T(128)S(1)} %fusion.11.lev, f32[5,64,8,128]{3,2,1,0:T(8,128)S(1)} %smooth_five.6.x, f32[64,8,128]{2,1,0:T(8,128)S(1)} %bitcast.93, f32[64,8,128]{2,1,0:T(8,128)S(1)} %bitcast.98, f32[64,8,128]{2,1,0:T(8,128)S(1)} %copy-done.11, f32[64,8,128]{2,1,0:T(8,128)S(1)} %copy-done.8, ...), custom_call_target="tpu_custom_call" | custom-call | flops 19660800 | bytes 5242880 | tf_op jit(solution)/shard_map/smooth_five/pallas_call | solution.py:85
  144.7 36.8 %psum.21 = f32[2]{0:T(128)S(1)} all-reduce(f32[2]{0:T(128)S(1)} %pad_maximum_fusion.2), channel_id=1, replica_groups=mesh['lon'=8,'lat'=4] {'lon','lat'}, use_global_device_ids=true, to_apply=%region_3.4 | all-reduce | flops 2 | bytes 16 | tf_op jit(solution)/shard_map/psum | solution.py:186
  184.0 3.3 multiply_reduce_fusion
  187.3 41.5 %psum.22 = f32[]{:T(128)} all-reduce(f32[]{:T(128)} %get-tuple-element.4), channel_id=1, replica_groups=mesh['lon'=8,'lat'=4] {'lon','lat'}, use_global_device_ids=true, to_apply=%region_5.6 | all-reduce | flops 1 | bytes 8 | tf_op jit(solution)/shard_map/psum | solution.py:193
  234.2 20.4 %smooth_five.8 = f32[5,64,8,128]{3,2,1,0:T(8,128)S(1)} custom-call(f32[5]{0:T(128)S(1)} %fusion.11.lev, f32[5,64,8,128]{3,2,1,0:T(8,128)S(1)} %copy-done, f32[64,8,128]{2,1,0:T(8,128)S(1)} %bitcast.94, f32[64,8,128]{2,1,0:T(8,128)S(1)} %bitcast.99, f32[64,8,128]{2,1,0:T(8,128)S(1)} %copy-done.12, f32[64,8,128]{2,1,0:T(8,128)S(1)} %copy-done.9, ...), custom_call_target="tpu_custom_call" | custom-call | flops 19660800 | bytes 5242880 | tf_op jit(solution)/shard_map/smooth_five/pallas_call | solution.py:85
  254.6 1.3 add_reduce_fusion
  255.9 20.4 %smooth_five.9 = f32[5,64,8,128]{3,2,1,0:T(8,128)S(1)} custom-call(f32[5]{0:T(128)S(1)} %fusion.11.lev, f32[5,64,8,128]{3,2,1,0:T(8,128)S(1)} %get-tuple-element.3.x, f32[64,8,128]{2,1,0:T(8,128)S(1)} %bitcast.95, f32[64,8,128]{2,1,0:T(8,128)S(1)} %bitcast.100, f32[64,8,128]{2,1,0:T(8,128)S(1)} %copy-done.12, f32[64,8,128]{2,1,0:T(8,128)S(1)} %copy-done.9, ...), custom_call_target="tpu_custom_call" | custom-call | flops 19660800 | bytes 5242880 | tf_op jit(solution)/shard_map/smooth_five/pallas_call | solution.py:85
  277.5 39.9 %psum.23 = f32[]{:T(128)} all-reduce(f32[]{:T(128)} %get-tuple-element.2), channel_id=1, replica_groups=mesh['lon'=8,'lat'=4] {'lon','lat'}, use_global_device_ids=true, to_apply=%region_7.8 | all-reduce | flops 1 | bytes 8 | tf_op jit(solution)/shard_map/psum | solution.py:198
  318.7 2.8 multiply_subtract_fusion
  321.5 1.3 copy.40
  322.8 4.5 %all-to-all-start.1 = ((f32[32,5,16,128]{3,2,1,0:T(8,128)}), f32[32,5,16,128]{3,2,1,0:T(8,128)S(1)}, u32[]{:S(2)}, u32[]{:S(2)}) async-start(f32[32,5,16,128]{3,2,1,0:T(8,128)} %bitcast.31), calls=%async_computation.1 | async-start | bytes 2621440 | tf_op jit(solution)/shard_map/all_to_all | solution.py:205
  327.3 1.3 copy.41
  328.6 30.5 %all-to-all-done.1 = f32[32,5,16,128]{3,2,1,0:T(8,128)S(1)} async-done(((f32[32,5,16,128]{3,2,1,0:T(8,128)}), f32[32,5,16,128]{3,2,1,0:T(8,128)S(1)}, u32[]{:S(2)}, u32[]{:S(2)}) %all-to-all-start.1) | async-done | bytes 1310752 | tf_op jit(solution)/shard_map/all_to_all | solution.py:205
  359.1 3.6 all-to-all-start.2
  363.8 30.7 %all-to-all-done.2 = f32[32,5,16,128]{3,2,1,0:T(8,128)S(1)} async-done(((f32[32,5,16,128]{3,2,1,0:T(8,128)}), f32[32,5,16,128]{3,2,1,0:T(8,128)S(1)}, u32[]{:S(2)}, u32[]{:S(2)}) %all-to-all-start.2) | async-done | bytes 1310752 | tf_op jit(solution)/shard_map/all_to_all | solution.py:205
  (100 shorter events, 26.1 us)
Async XLA Ops:
  2.3 58.6 %all-to-all-start = ((f32[32,5,128]{2,1,0:T(8,128)}), f32[32,5,128]{2,1,0:T(8,128)S(1)}, u32[]{:S(2)}, u32[]{:S(2)}) async-start(f32[32,5,128]{2,1,0:T(8,128)} %reshape.144), calls=%async_computation | async-start | bytes 262144 | tf_op jit(solution)/shard_map/all_to_all | solution.py:128
  57.7 17.1 %copy-start.15 = (f32[1,4,16,8,128]{4,3,2,1,0:T(8,128)}, f32[1,4,16,8,128]{4,3,2,1,0:T(8,128)S(1)}, u32[]{:S(2)}) copy-start(f32[1,4,16,8,128]{4,3,2,1,0:T(8,128)S(1)} %copy.31) | copy-start | bytes 786436
  60.4 14.6 %copy-start.4 = (f32[64,8,128]{2,1,0:T(8,128)}, f32[64,8,128]{2,1,0:T(8,128)S(1)}, u32[]{:S(2)}) copy-start(f32[64,8,128]{2,1,0:T(8,128)S(1)} %get-tuple-element.15.dn) | copy-start | bytes 786436
  60.4 14.6 %copy-start.7 = (f32[64,8,128]{2,1,0:T(8,128)}, f32[64,8,128]{2,1,0:T(8,128)S(1)}, u32[]{:S(2)}) copy-start(f32[64,8,128]{2,1,0:T(8,128)S(1)} %get-tuple-element.16.de) | copy-start | bytes 786436
  60.4 14.6 %copy-start.10 = (f32[64,8,128]{2,1,0:T(8,128)}, f32[64,8,128]{2,1,0:T(8,128)S(1)}, u32[]{:S(2)}) copy-start(f32[64,8,128]{2,1,0:T(8,128)S(1)} %get-tuple-element.26.kn) | copy-start | bytes 786436
  74.6 44.9 %copy-start.19 = (f32[1,4,16,8,128]{4,3,2,0,1:T(8,128)}, f32[1,4,16,8,128]{4,3,2,0,1:T(8,128)S(1)}, u32[]{:S(2)}) copy-start(f32[1,4,16,8,128]{4,3,2,0,1:T(8,128)S(1)} %slice.116) | copy-start | bytes 786436
  95.4 1.0 copy-start.5
  96.3 0.9 copy-start.8
  97.3 0.9 copy-start.11
  118.6 1.0 copy-start.16
  142.5 1.1 copy-start.2
  143.6 1.1 copy-start.13
  230.1 1.3 copy-start
  231.4 0.9 copy-start.6
  232.3 0.9 copy-start.9
  233.3 0.9 copy-start.12
  234.2 20.4 %copy-start.17 = (f32[1,4,16,8,128]{4,3,2,1,0:T(8,128)S(1)}, f32[1,4,16,8,128]{4,3,2,1,0:T(8,128)}, u32[]{:S(2)}) copy-start(f32[1,4,16,8,128]{4,3,2,1,0:T(8,128)} %copy-done.15) | copy-start | bytes 786436
  234.2 20.4 %copy-start.20 = (f32[1,4,16,8,128]{4,3,2,0,1:T(8,128)S(1)}, f32[1,4,16,8,128]{4,3,2,0,1:T(8,128)}, u32[]{:S(2)}) copy-start(f32[1,4,16,8,128]{4,3,2,0,1:T(8,128)} %copy-done.19) | copy-start | bytes 786436
  254.6 1.3 copy-start.3
  255.9 62.8 %copy-start.1 = (f32[5,64,8,128]{3,2,1,0:T(8,128)S(1)}, f32[5,64,8,128]{3,2,1,0:T(8,128)}, u32[]{:S(2)}) copy-start(f32[5,64,8,128]{3,2,1,0:T(8,128)} %get-tuple-element.5.x) | copy-start | bytes 3932164
  276.4 1.1 copy-start.14
  322.8 4.5 %copy-start.18 = (f32[5,64,8,128]{3,2,1,0:T(8,128)S(1)}, f32[5,64,8,128]{3,2,1,0:T(8,128)}, u32[]{:S(2)}) copy-start(f32[5,64,8,128]{3,2,1,0:T(8,128)} %get-tuple-element.6) | copy-start | bytes 3932164
  322.8 36.3 %all-to-all-start.1 = ((f32[32,5,16,128]{3,2,1,0:T(8,128)}), f32[32,5,16,128]{3,2,1,0:T(8,128)S(1)}, u32[]{:S(2)}, u32[]{:S(2)}) async-start(f32[32,5,16,128]{3,2,1,0:T(8,128)} %bitcast.31), calls=%async_computation.1 | async-start | bytes 2621440 | tf_op jit(solution)/shard_map/all_to_all | solution.py:205
  359.1 35.4 %all-to-all-start.2 = ((f32[32,5,16,128]{3,2,1,0:T(8,128)}), f32[32,5,16,128]{3,2,1,0:T(8,128)S(1)}, u32[]{:S(2)}, u32[]{:S(2)}) async-start(f32[32,5,16,128]{3,2,1,0:T(8,128)} %bitcast.35), calls=%async_computation.2 | async-start | bytes 2621440 | tf_op jit(solution)/shard_map/all_to_all | solution.py:205
  (4 other events, 3.0 us)

commit v2 on v1

--- a/solution.py
+++ b/solution.py
@@ -9,16 +9,17 @@
 
 NZ = 75
 AXES = ("lon", "lat")
-
-
-def smooth_kernel(lev, x, ke, kw, kn, de, dw, dn, *rest):
+BLOCK = 64
+
+
+def smooth_kernel(block, lev, x, ke, kw, kn, de, dw, dn, *rest):
     if len(rest) == 8:
         gain, out, va, vb, fe, fw, fn, dd = rest
     else:
         gain = None
         out, va, vb, fe, fw, fn, dd = rest
     channels, rows, tiles, lanes = x.shape
-    block = 8
+
     blocks = rows // block
     zero = jnp.zeros((tiles, lanes), jnp.float32)
     for c in range(channels):
@@ -56,10 +57,10 @@
             r = (i % blocks) * block
             here = pl.ds(r, block)
             centre = src[c, pl.ds(r + 1, block)]
-            east = pltpu.roll(centre, lanes - 1, 2)
-            east = jnp.where(lane == lanes - 1, pltpu.roll(east, tiles - 1, 1), east)
-            west = pltpu.roll(centre, 1, 2)
-            west = jnp.where(lane == 0, pltpu.roll(west, 1, 1), west)
+            east = jnp.where(lane == 0, pltpu.roll(centre, tiles - 1, 1), centre)
+            east = pltpu.roll(east, lanes - 1, 2)
+            west = jnp.where(lane == lanes - 1, pltpu.roll(centre, 1, 1), centre)
+            west = pltpu.roll(west, 1, 2)
             new = dd[c, here] * centre + fe[c, here] * east + fw[c, here] * west
             new = new + fn[c, pl.ds(r + 1, block)] * src[c, pl.ds(r + 2, block)]
             new = new + fn[c, here] * src[c, here]
@@ -83,7 +84,7 @@
     padded = pltpu.VMEM((channels, rows + 2, tiles, lanes), jnp.float32)
     cells = channels * rows * tiles * lanes
     return pl.pallas_call(
-        smooth_kernel,
+        functools.partial(smooth_kernel, BLOCK),
         out_shape=jax.ShapeDtypeStruct(x.shape, jnp.float32),
         in_specs=[pl.BlockSpec(memory_space=pltpu.SMEM)] + [vmem] * (len(operands) - 1),
         out_specs=vmem,
@@ -118,16 +119,19 @@
             obs_lat.astype(jnp.float32),
         ]
     ).reshape(-1, lanes)
-    everywhere = lax.all_gather(packed, AXES, axis=0, tiled=False)
+    misfit = jnp.pad(obs_precision[:, None] * innovation, ((0, spare), (0, 0)))
+    misfit = misfit.reshape(devices, channels, listed)
+    sent = jnp.concatenate(
+        [jnp.broadcast_to(packed[None], (devices,) + packed.shape), misfit], axis=1
+    )
+    everywhere = lax.all_to_all(sent, AXES, split_axis=0, concat_axis=0, tiled=True)
+    misfit = everywhere[:, packed.shape[0] :]
+    everywhere = everywhere[:, : packed.shape[0]]
     maps = everywhere[:, : 3 * rows].reshape(tiles, bands, 3, rows, lanes)
     maps = maps.transpose(2, 1, 3, 0, 4).reshape(3, bands * rows, tiles, lanes)
     places = everywhere[:, 3 * rows :].reshape(tiles, bands, 2, listed)
     places = places.transpose(2, 1, 0, 3).reshape(2, bands, tiles * listed)
 
-    misfit = jnp.pad(obs_precision[:, None] * innovation, ((0, spare), (0, 0)))
-    misfit = lax.all_to_all(
-        misfit.reshape(devices, channels, listed), AXES, split_axis=0, concat_axis=0, tiled=True
-    )
     misfit = misfit.reshape(tiles, bands, channels, listed).transpose(1, 2, 0, 3)
     misfit = misfit.reshape(bands, channels, tiles * listed)
 
@@ -181,21 +185,25 @@
     scaled_wet = scale[:, None, None, None] * wet
     gain = scaled_wet * (scale * weight)[:, None, None, None] * cells[channels][None]
 
+    def everyone(partial):
+        wide = jnp.broadcast_to(partial[None, ..., None], (devices,) + partial.shape + (lanes,))
+        return lax.all_to_all(wide, AXES, split_axis=0, concat_axis=0, tiled=True).sum(0)[..., 0]
+
     rhs = smooth_five(scaled_wet * cells[:channels], faces, lev)
     q_one = smooth_five(rhs, faces, lev)
-    sums = lax.psum(
-        jnp.stack([jnp.sum(rhs * rhs), jnp.sum(q_one * q_one * gain)]), AXES
+    sums = everyone(
+        jnp.stack([jnp.sum(rhs * rhs), jnp.sum(q_one * q_one * gain)])
     )
     s_one = smooth_five(q_one, faces, lev, gain)
     norm_zero = sums[0]
     alpha_one = norm_zero / (norm_zero + sums[1])
     r_one = rhs - alpha_one * (rhs + s_one)
-    norm_one = lax.psum(jnp.sum(r_one * r_one), AXES)
+    norm_one = everyone(jnp.sum(r_one * r_one))
     t_one = smooth_five(r_one, faces, lev)
     beta = norm_one / norm_zero
     p_two = r_one + beta * rhs
     q_two = t_one + beta * q_one
-    curve = lax.psum(jnp.sum(p_two * p_two + q_two * q_two * gain), AXES)
+    curve = everyone(jnp.sum(p_two * p_two + q_two * q_two * gain))
     s_two = smooth_five(q_two, faces, lev, gain)
     alpha_two = norm_one / curve
 

time: 397 us -> 220 us (0.55)
  blocking collectives: 162 us -> 0 us
  Pallas kernels: 102 us -> 36.5 us
  waiting for transfers between devices: 61.2 us -> 84.5 us
  starting transfers between devices: 15.4 us -> 32 us
  local copies, waits for them, and re-layouts: 26.4 us -> 35.5 us
    psum x3 -> x0, blocking collectives: 118 us -> none  [the longest x1 41.5 us: local(): norm_one = lax.psum(jnp.sum(r_one * r_one), AXES)]
    pallas_call x5, Pallas kernels: 102 us -> 36.5 us  [smooth_five(): pl.pallas_call(functools.partial(smooth_kernel, BLOCK), out_shape=jax.Sha...]
    all_gather x1 -> x0, blocking collectives: 44.3 us -> none  [local(): everywhere = lax.all_gather(packed, AXES, axis=0, tiled=False)]
    all_to_all x1 -> x4, waiting for transfers between devices: 0.01 us -> 23.3 us  [the longest x1 23.3 us: local(): lax.all_to_all(sent, AXES, split_axis=0, concat_axis=0, tiled=True)]
    all_to_all x1 -> x4, starting transfers between devices: 7.33 us -> 22.6 us  [the longest x3 15.3 us: everyone(): lax.all_to_all(wide, AXES, split_axis=0, concat_axis=0, tiled=True).sum(0)]
    unnamed x59 -> x66, local copies, waits for them, and re-layouts: 16.1 us -> 23.4 us
  transfers between devices with their start and end apart: 3 -> 6, of which waited for: 2 -> 3; matrix products, arithmetic and copies ran while one was open for 2% -> 1% of each run, Pallas kernels for 0% -> 10%
where the time goes in v2:
time: 220 us; the launch traced here: 218 us
  waiting for transfers between devices  84.5 us (38%)
  Pallas kernels  36.5 us (17%)
  local copies, waits for them, and re-layouts  35.5 us (16%)
  starting transfers between devices  32 us (15%)
  other arithmetic  22.9 us (10%)
  between operations  3.86 us (2%)
  matrix products  2.89 us (1%)
    all_to_all x2, waiting for transfers between devices, home(): moved = lax.all_to_all(split, AXES, split_axis=0, concat_axis=0, tiled=True)  61.3 us
    pallas_call x5, Pallas kernels, smooth_five(): pl.pallas_call(functools.partial(smooth_kernel, BLOCK), out_shape=jax.Sha...  36.5 us
    unnamed x66, local copies, waits for them, and re-layouts  23.4 us
    all_to_all x1, waiting for transfers between devices, local(): lax.all_to_all(sent, AXES, split_axis=0, concat_axis=0, tiled=True)  23.3 us
    all_to_all x3, starting transfers between devices, everyone(): lax.all_to_all(wide, AXES, split_axis=0, concat_axis=0, tiled=True).sum(0)  15.3 us
    all_to_all x2, starting transfers between devices, home(): moved = lax.all_to_all(split, AXES, split_axis=0, concat_axis=0, tiled=True)  9.44 us
    all_to_all x1, starting transfers between devices, local(): lax.all_to_all(sent, AXES, split_axis=0, concat_axis=0, tiled=True)  7.33 us
  transfers between devices with their start and end apart: 6, of which 3 were waited for; matrix products, arithmetic and copies ran while one was open for 1% of the time, Pallas kernels for 10%

profile of v2, /device:TPU:0, one launch (start us, length us, event | category | flops | bytes accessed | tf_op | source)
XLA Modules:
  0.0 218.3 jit_solution(11436452970649150744)
XLA Ops:
  6.1 7.3 %all-to-all-start = ((f32[32,55,128]{2,1,0:T(8,128)}), f32[32,55,128]{2,1,0:T(8,128)S(1)}, u32[]{:S(2)}, u32[]{:S(2)}) async-start(f32[32,55,128]{2,1,0:T(8,128)} %pad_maximum_fusion), calls=%async_computation | async-start | bytes 1835008 | tf_op jit(solution)/shard_map/all_to_all | solution.py:127
  13.6 23.3 %all-to-all-done = f32[32,55,128]{2,1,0:T(8,128)S(1)} async-done(((f32[32,55,128]{2,1,0:T(8,128)}), f32[32,55,128]{2,1,0:T(8,128)S(1)}, u32[]{:S(2)}, u32[]{:S(2)}) %all-to-all-start) | async-done | bytes 901152 | tf_op jit(solution)/shard_map/all_to_all | solution.py:127
  40.2 2.9 %fusion = f32[4,288,1024]{2,1,0:T(8,128)S(1)} fusion(bf16[4,288,1024]{2,1,0:T(8,128)(2,1)S(1)} %bitcast.126, f32[4,1024]{1,0:T(4,128)S(1)} %get-tuple-element.20), kind=kOutput, calls=%fused_computation.1 | convolution fusion | flops 2420113408 | bytes 7094272 | tf_op jit(solution)/shard_map/dot_general | solution.py:176
  43.1 3.3 %copy.70 = f32[144,8,8,128]{3,2,1,0:T(8,128)} copy(f32[144,8,8,128]{3,1,2,0:T(8,128)S(1)} %bitcast.124) | data formatting | bytes 9437184
  46.3 2.9 %reduce_sum.72 = f32[4,6,16,8,128]{4,3,2,1,0:T(8,128)S(1)} reduce(f32[4,3,6,16,8,128]{5,4,3,2,1,0:T(8,128)} %bitcast.109, f32[]{:T(128)} %constant.37.clone.1), dimensions={1}, to_apply=%region_0.1 | reduce | flops 786432 | bytes 6291460 | tf_op jit(solution)/shard_map/reduce_sum | solution.py:182
  52.3 7.3 %smooth_five.5.x = f32[5,64,8,128]{3,2,1,0:T(8,128)S(1)} custom-call(f32[5]{0:T(128)S(1)} %fusion.11.lev, f32[5,64,8,128]{3,2,1,0:T(8,128)S(1)} %select_multiply_fusion.1.x, f32[64,8,128]{2,1,0:T(8,128)S(1)} %bitcast.94, f32[64,8,128]{2,1,0:T(8,128)S(1)} %bitcast.99, f32[64,8,128]{2,1,0:T(8,128)S(1)} %get-tuple-element.26.kn, ...), custom_call_target="tpu_custom_call" | custom-call | flops 19660800 | bytes 5242880 | tf_op jit(solution)/shard_map/smooth_five/pallas_call | solution.py:86
  59.7 7.3 %smooth_five.6.x = f32[5,64,8,128]{3,2,1,0:T(8,128)S(1)} custom-call(f32[5]{0:T(128)S(1)} %fusion.11.lev, f32[5,64,8,128]{3,2,1,0:T(8,128)S(1)} %smooth_five.5.x, f32[64,8,128]{2,1,0:T(8,128)S(1)} %bitcast.95, f32[64,8,128]{2,1,0:T(8,128)S(1)} %bitcast.100, f32[64,8,128]{2,1,0:T(8,128)S(1)} %get-tuple-element.26.kn, f32[64,8,128]{2,1,0:T(8,128)S(1)} %get-tuple-element.16.de, ...), custom_call_target="tpu_custom_call" | custom-call | flops 19660800 | bytes 5242880 | tf_op jit(solution)/shard_map/smooth_five/pallas_call | solution.py:86
  68.0 2.1 multiply_reduce_fusion.1
  70.1 1.4 pad_maximum_fusion.3
  72.2 3.8 %all-to-all-start.1 = ((f32[32,2,128]{2,1,0:T(2,128)}), f32[32,2,128]{2,1,0:T(2,128)S(1)}, u32[]{:S(2)}, u32[]{:S(2)}) async-start(f32[32,2,128]{2,1,0:T(2,128)} %broadcast_in_dim.76), calls=%async_computation.1 | async-start | bytes 65536 | tf_op jit(solution)/shard_map/all_to_all | solution.py:190
  80.1 7.3 %smooth_five.7 = f32[5,64,8,128]{3,2,1,0:T(8,128)S(1)} custom-call(f32[5]{0:T(128)S(1)} %fusion.11.lev, f32[5,64,8,128]{3,2,1,0:T(8,128)S(1)} %smooth_five.6.x, f32[64,8,128]{2,1,0:T(8,128)S(1)} %bitcast.96, f32[64,8,128]{2,1,0:T(8,128)S(1)} %bitcast.101, f32[64,8,128]{2,1,0:T(8,128)S(1)} %copy-done.13, f32[64,8,128]{2,1,0:T(8,128)S(1)} %copy-done.9, ...), custom_call_target="tpu_custom_call" | custom-call | flops 19660800 | bytes 5242880 | tf_op jit(solution)/shard_map/smooth_five/pallas_call | solution.py:86
  91.1 3.3 %multiply_reduce_fusion = (f32[]{:T(128)}, f32[5,64,8,128]{3,2,1,0:T(8,128)}) fusion(f32[5,64,8,128]{3,2,1,0:T(8,128)S(1)} %smooth_five.5.x, f32[5,64,8,128]{3,2,1,0:T(8,128)} %copy-done.16, f32[]{:T(128)S(6)} %div.9), kind=kLoop, calls=%fused_computation.12 | loop fusion | flops 1638399 | bytes 3932168 | tf_op jit(solution)/shard_map/reduce_sum | solution.py:201
  95.7 5.7 %all-to-all-start.2 = ((f32[32,1,128]{2,1,0:T(1,128)}), f32[32,1,128]{2,1,0:T(1,128)S(1)}, u32[]{:S(2)}, u32[]{:S(2)}) async-start(f32[32,1,128]{2,1,0:T(1,128)} %broadcast_in_dim.77), calls=%async_computation.2 | async-start | bytes 32768 | tf_op jit(solution)/shard_map/all_to_all | solution.py:190
  105.5 7.3 %smooth_five.8 = f32[5,64,8,128]{3,2,1,0:T(8,128)S(1)} custom-call(f32[5]{0:T(128)S(1)} %fusion.11.lev, f32[5,64,8,128]{3,2,1,0:T(8,128)S(1)} %copy-done, f32[64,8,128]{2,1,0:T(8,128)S(1)} %bitcast.97, f32[64,8,128]{2,1,0:T(8,128)S(1)} %bitcast.102, f32[64,8,128]{2,1,0:T(8,128)S(1)} %copy-done.14, f32[64,8,128]{2,1,0:T(8,128)S(1)} %copy-done.10, ...), custom_call_target="tpu_custom_call" | custom-call | flops 19660800 | bytes 5242880 | tf_op jit(solution)/shard_map/smooth_five/pallas_call | solution.py:86
  114.7 4.2 %add_reduce_fusion = (f32[]{:T(128)}, f32[5,64,8,128]{3,2,1,0:T(8,128)}) fusion(f32[5,64,8,128]{3,2,1,0:T(8,128)} %get-tuple-element.5.x, f32[5,64,8,128]{3,2,1,0:T(8,128)S(1)} %smooth_five.5.x, f32[]{:T(128)S(6)} %div.10, f32[64,8,128]{2,1,0:T(8,128)} %bitcast.128, f32[5]{0:T(128)S(1)} %get-tuple-element.24, f32[5]{0:T(128)S(1)} %get-tuple-element.25, ...), kind=kLoop, calls=%fused_computation.9 | loop fusion | flops 4259839 | bytes 7077956 | tf_op jit(solution)/shard_map/reduce_sum | solution.py:206
  120.1 5.8 %all-to-all-start.3 = ((f32[32,1,128]{2,1,0:T(1,128)}), f32[32,1,128]{2,1,0:T(1,128)S(1)}, u32[]{:S(2)}, u32[]{:S(2)}) async-start(f32[32,1,128]{2,1,0:T(1,128)} %broadcast_in_dim.78), calls=%async_computation.3 | async-start | bytes 32768 | tf_op jit(solution)/shard_map/all_to_all | solution.py:190
  130.1 1.3 copy-done.19
  131.4 7.3 %smooth_five.9 = f32[5,64,8,128]{3,2,1,0:T(8,128)S(1)} custom-call(f32[5]{0:T(128)S(1)} %fusion.11.lev, f32[5,64,8,128]{3,2,1,0:T(8,128)S(1)} %copy-done.19, f32[64,8,128]{2,1,0:T(8,128)S(1)} %bitcast.98, f32[64,8,128]{2,1,0:T(8,128)S(1)} %bitcast.103, f32[64,8,128]{2,1,0:T(8,128)S(1)} %copy-done.15, f32[64,8,128]{2,1,0:T(8,128)S(1)} %copy-done.11, ...), custom_call_target="tpu_custom_call" | custom-call | flops 19660800 | bytes 5242880 | tf_op jit(solution)/shard_map/smooth_five/pallas_call | solution.py:86
  140.0 2.7 %multiply_subtract_fusion = (f32[5,64,8,128]{3,2,1,0:T(8,128)}, f32[5,64,8,128]{3,2,1,0:T(8,128)S(1)}) fusion(f32[5,64,8,128]{3,2,1,0:T(8,128)S(1)} %copy-done.1, f32[5,64,8,128]{3,2,1,0:T(8,128)} %copy-done.18, f32[]{:T(128)S(6)} %div.11, f32[5,64,8,128]{3,2,1,0:T(8,128)S(1)} %smooth_five.5.x, f32[]{:T(128)S(6)} %div.10, f32[]{:T(128)S(6)} %div.9), kind=kLoop, calls=%fused_computation.7 | loop fusion | flops 2621440 | bytes 6553612 | tf_op jit(solution)/shard_map/sub | solution.py:217
  142.7 1.3 copy.65
  144.0 5.8 %all-to-all-start.4 = ((f32[32,5,16,128]{3,2,1,0:T(8,128)}), f32[32,5,16,128]{3,2,1,0:T(8,128)S(1)}, u32[]{:S(2)}, u32[]{:S(2)}) async-start(f32[32,5,16,128]{3,2,1,0:T(8,128)} %bitcast.36), calls=%async_computation.4 | async-start | bytes 2621440 | tf_op jit(solution)/shard_map/all_to_all | solution.py:213
  151.2 30.5 %all-to-all-done.4 = f32[32,5,16,128]{3,2,1,0:T(8,128)S(1)} async-done(((f32[32,5,16,128]{3,2,1,0:T(8,128)}), f32[32,5,16,128]{3,2,1,0:T(8,128)S(1)}, u32[]{:S(2)}, u32[]{:S(2)}) %all-to-all-start.4) | async-done | bytes 1310752 | tf_op jit(solution)/shard_map/all_to_all | solution.py:213
  181.7 3.6 %all-to-all-start.5 = ((f32[32,5,16,128]{3,2,1,0:T(8,128)}), f32[32,5,16,128]{3,2,1,0:T(8,128)S(1)}, u32[]{:S(2)}, u32[]{:S(2)}) async-start(f32[32,5,16,128]{3,2,1,0:T(8,128)} %bitcast.40), calls=%async_computation.5 | async-start | bytes 2621440 | tf_op jit(solution)/shard_map/all_to_all | solution.py:213
  186.4 30.7 %all-to-all-done.5 = f32[32,5,16,128]{3,2,1,0:T(8,128)S(1)} async-done(((f32[32,5,16,128]{3,2,1,0:T(8,128)}), f32[32,5,16,128]{3,2,1,0:T(8,128)S(1)}, u32[]{:S(2)}, u32[]{:S(2)}) %all-to-all-start.5) | async-done | bytes 1310752 | tf_op jit(solution)/shard_map/all_to_all | solution.py:213
  (118 shorter events, 35.9 us)
Async XLA Ops:
  6.1 7.4 %copy-start.27 = (f32[151]{0:T(256)S(1)}, f32[151]{0:T(256)}, u32[]{:S(2)}) copy-start(f32[151]{0:T(256)} %param.13) | copy-start | bytes 1816
  6.1 7.4 %copy-start.28 = (f32[151]{0:T(256)S(1)}, f32[151]{0:T(256)}, u32[]{:S(2)}) copy-start(f32[151]{0:T(256)} %param.12) | copy-start | bytes 1816
  6.1 30.7 %all-to-all-start = ((f32[32,55,128]{2,1,0:T(8,128)}), f32[32,55,128]{2,1,0:T(8,128)S(1)}, u32[]{:S(2)}, u32[]{:S(2)}) async-start(f32[32,55,128]{2,1,0:T(8,128)} %pad_maximum_fusion), calls=%async_computation | async-start | bytes 1835008 | tf_op jit(solution)/shard_map/all_to_all | solution.py:127
  37.9 13.6 %copy-start.20 = (f32[1,4,16,8,128]{4,3,2,1,0:T(8,128)}, f32[1,4,16,8,128]{4,3,2,1,0:T(8,128)S(1)}, u32[]{:S(2)}) copy-start(f32[1,4,16,8,128]{4,3,2,1,0:T(8,128)S(1)} %copy.53) | copy-start | bytes 786436
  49.4 18.6 %copy-start.23 = (f32[1,4,16,8,128]{4,3,2,0,1:T(8,128)}, f32[1,4,16,8,128]{4,3,2,0,1:T(8,128)S(1)}, u32[]{:S(2)}) copy-start(f32[1,4,16,8,128]{4,3,2,0,1:T(8,128)S(1)} %slice.137) | copy-start | bytes 786436
  49.8 1.0 copy-start.24
  52.3 7.3 %copy-start.4 = (f32[64,8,128]{2,1,0:T(8,128)}, f32[64,8,128]{2,1,0:T(8,128)S(1)}, u32[]{:S(2)}) copy-start(f32[64,8,128]{2,1,0:T(8,128)S(1)} %get-tuple-element.15.dn) | copy-start | bytes 786436
  52.3 7.3 %copy-start.8 = (f32[64,8,128]{2,1,0:T(8,128)}, f32[64,8,128]{2,1,0:T(8,128)S(1)}, u32[]{:S(2)}) copy-start(f32[64,8,128]{2,1,0:T(8,128)S(1)} %get-tuple-element.16.de) | copy-start | bytes 786436
  52.3 7.3 %copy-start.12 = (f32[64,8,128]{2,1,0:T(8,128)}, f32[64,8,128]{2,1,0:T(8,128)S(1)}, u32[]{:S(2)}) copy-start(f32[64,8,128]{2,1,0:T(8,128)S(1)} %get-tuple-element.26.kn) | copy-start | bytes 786436
  67.0 1.0 copy-start.21
  72.2 16.4 %all-to-all-start.1 = ((f32[32,2,128]{2,1,0:T(2,128)}), f32[32,2,128]{2,1,0:T(2,128)S(1)}, u32[]{:S(2)}, u32[]{:S(2)}) async-start(f32[32,2,128]{2,1,0:T(2,128)} %broadcast_in_dim.76), calls=%async_computation.1 | async-start | bytes 65536 | tf_op jit(solution)/shard_map/all_to_all | solution.py:190
  76.0 1.3 copy-start.2
  87.5 1.1 copy-start.16
  95.7 18.2 %all-to-all-start.2 = ((f32[32,1,128]{2,1,0:T(1,128)}), f32[32,1,128]{2,1,0:T(1,128)S(1)}, u32[]{:S(2)}, u32[]{:S(2)}) async-start(f32[32,1,128]{2,1,0:T(1,128)} %broadcast_in_dim.77), calls=%async_computation.2 | async-start | bytes 32768 | tf_op jit(solution)/shard_map/all_to_all | solution.py:190
  101.4 1.3 copy-start
  112.8 1.1 copy-start.17
  120.1 19.8 %all-to-all-start.3 = ((f32[32,1,128]{2,1,0:T(1,128)}), f32[32,1,128]{2,1,0:T(1,128)S(1)}, u32[]{:S(2)}, u32[]{:S(2)}) async-start(f32[32,1,128]{2,1,0:T(1,128)} %broadcast_in_dim.78), calls=%async_computation.3 | async-start | bytes 32768 | tf_op jit(solution)/shard_map/all_to_all | solution.py:190
  125.9 1.3 copy-start.3
  130.1 1.3 copy-start.19
  131.4 8.5 %copy-start.1 = (f32[5,64,8,128]{3,2,1,0:T(8,128)S(1)}, f32[5,64,8,128]{3,2,1,0:T(8,128)}, u32[]{:S(2)}) copy-start(f32[5,64,8,128]{3,2,1,0:T(8,128)} %get-tuple-element.5.x) | copy-start | bytes 3932164
  138.8 1.1 copy-start.18
  144.0 5.8 %copy-start.22 = (f32[5,64,8,128]{3,2,1,0:T(8,128)S(1)}, f32[5,64,8,128]{3,2,1,0:T(8,128)}, u32[]{:S(2)}) copy-start(f32[5,64,8,128]{3,2,1,0:T(8,128)} %get-tuple-element.6) | copy-start | bytes 3932164
  144.0 37.7 %all-to-all-start.4 = ((f32[32,5,16,128]{3,2,1,0:T(8,128)}), f32[32,5,16,128]{3,2,1,0:T(8,128)S(1)}, u32[]{:S(2)}, u32[]{:S(2)}) async-start(f32[32,5,16,128]{3,2,1,0:T(8,128)} %bitcast.36), calls=%async_computation.4 | async-start | bytes 2621440 | tf_op jit(solution)/shard_map/all_to_all | solution.py:213
  181.7 35.4 %all-to-all-start.5 = ((f32[32,5,16,128]{3,2,1,0:T(8,128)}), f32[32,5,16,128]{3,2,1,0:T(8,128)S(1)}, u32[]{:S(2)}, u32[]{:S(2)}) async-start(f32[32,5,16,128]{3,2,1,0:T(8,128)} %bitcast.40), calls=%async_computation.5 | async-start | bytes 2621440 | tf_op jit(solution)/shard_map/all_to_all | solution.py:213
  (11 other events, 10.5 us)

commit v3 on v2

v3 whole, which is shorter than its diff:
```python
import functools

import jax
import jax.numpy as jnp
from jax import lax
from jax.experimental import pallas as pl
from jax.experimental.pallas import tpu as pltpu
from jax.sharding import PartitionSpec as P

NZ = 75
AXES = ("lon", "lat")


def smooth_kernel(stage, lev, scalar, ke, kw, kn, de, dw, dn, *rest):
    counts = {"first": 1, "curve": 2, "next": 4, "last": 3}
    fields, rest = rest[: counts[stage]], rest[counts[stage] :]
    outs, (va, vb, fe, fw, fn, dd) = rest[:-6], rest[-6:]
    channels, rows, tiles, lanes = fields[0].shape
    zero = jnp.zeros((tiles, lanes), jnp.float32)
    inner = pl.ds(1, rows)
    for c in range(channels):
        va[c, 0] = zero
        vb[c, 0] = zero
        va[c, rows + 1] = zero
        vb[c, rows + 1] = zero
        fn[c, 0] = zero

    def build(c, carry):
        level = lev[c]
        east = jnp.where(de[...] > level, ke[...], 0.0)
        west = jnp.where(dw[...] > level, kw[...], 0.0)
        north = jnp.where(dn[...] > level, kn[...], 0.0)
        fe[c] = east
        fw[c] = west
        fn[c, inner] = north
        south = fn[c, pl.ds(0, rows)]
        dd[c] = 1.0 - (east + west + north + south)
        return carry

    lax.fori_loop(0, channels, build, 0)
    lane = lax.broadcasted_iota(jnp.int32, (rows, tiles, lanes), 2)

    def step(src, dst, shift):
        def body(c, carry):
            centre = src[c, inner]
            east = jnp.where(lane == 0, pltpu.roll(centre, tiles - 1, 1), centre)
            east = pltpu.roll(east, lanes - 1, 2)
            west = jnp.where(lane == lanes - 1, pltpu.roll(centre, 1, 1), centre)
            west = pltpu.roll(west, 1, 2)
            new = dd[c] * centre + fe[c] * east + fw[c] * west
            new = new + fn[c, inner] * src[c, pl.ds(2, rows)]
            new = new + fn[c, pl.ds(0, rows)] * src[c, pl.ds(0, rows)]
            dst[c, pl.ds(shift, rows)] = new
            return carry

        lax.fori_loop(0, channels, body, 0)

    def five(dst):
        step(va, vb, 1)
        step(vb, va, 1)
        step(va, vb, 1)
        step(vb, va, 1)
        step(va, dst, 0)

    def each(body, sums):
        start = (zero,) * sums
        return lax.fori_loop(0, channels, body, start)

    if stage == "first":
        (x,) = fields
        (out,) = outs

        def load(c, carry):
            va[c, inner] = x[c]
            return carry

        each(load, 0)
        five(out)
    elif stage == "curve":
        rhs, gain = fields
        q_out, s_out, sums = outs

        def load(c, carry):
            cells = rhs[c]
            va[c, inner] = cells
            return (carry[0] + jnp.sum(cells * cells, 0),)

        (sums[0],) = each(load, 1)
        five(q_out)

        def weigh(c, carry):
            cells = q_out[c]
            gained = cells * gain[c]
            va[c, inner] = gained
            return (carry[0] + jnp.sum(cells * gained, 0),)

        (sums[1],) = each(weigh, 1)
        five(s_out)
    elif stage == "next":
        rhs, q_one, s_one, gain = fields
        r_out, t_out, sums = outs

        def load(c, carry):
            base = rhs[c]
            cells = base - scalar[0] * (base + s_one[c])
            va[c, inner] = cells
            r_out[c] = cells
            return (carry[0] + jnp.sum(cells * cells, 0), carry[1] + jnp.sum(cells * base, 0))

        sums[0], sums[1] = each(load, 2)
        five(t_out)

        def weigh(c, carry):
            cells = t_out[c]
            gained = cells * gain[c]
            return (
                carry[0] + jnp.sum(cells * gained, 0),
                carry[1] + jnp.sum(q_one[c] * gained, 0),
            )

        sums[2], sums[3] = each(weigh, 2)
    else:
        q_one, t_one, gain = fields
        (out,) = outs

        def load(c, carry):
            va[c, inner] = (t_one[c] + scalar[0] * q_one[c]) * gain[c]
            return carry

        each(load, 0)
        five(out)


def smooth(stage, lev, scalar, faces, *fields):
    channels, rows, tiles, lanes = fields[0].shape
    vmem = pl.BlockSpec(memory_space=pltpu.VMEM)
    smem = pl.BlockSpec(memory_space=pltpu.SMEM)
    outs, sums, rounds = {
        "first": (1, 0, 1),
        "curve": (2, 2, 2),
        "next": (2, 4, 1),
        "last": (1, 0, 1),
    }[stage]
    shapes = [jax.ShapeDtypeStruct(fields[0].shape, jnp.float32)] * outs
    if sums:
        shapes.append(jax.ShapeDtypeStruct((sums, tiles, lanes), jnp.float32))
    field = pltpu.VMEM((channels, rows, tiles, lanes), jnp.float32)
    padded = pltpu.VMEM((channels, rows + 2, tiles, lanes), jnp.float32)
    cells = channels * rows * tiles * lanes
    return pl.pallas_call(
        functools.partial(smooth_kernel, stage),
        out_shape=shapes,
        in_specs=[smem, smem] + [vmem] * (len(faces) + len(fields)),
        out_specs=[vmem] * len(shapes),
        scratch_shapes=[padded, padded, field, field, padded, field],
        cost_estimate=pl.CostEstimate(
            flops=60 * cells * rounds, bytes_accessed=16 * cells, transcendentals=0
        ),
        compiler_params=pltpu.CompilerParams(vmem_limit_bytes=48 * 1024 * 1024),
        name="smooth_" + stage,
    )(lev, jnp.reshape(scalar, (1,)), *faces, *fields)


def gather_kernel(reduce, tiles, bands, x, out, held, send, recv, own_sem):
    lon, lat = lax.axis_index("lon"), lax.axis_index("lat")
    beside = [(lon, lax.rem(lat + k, bands)) for k in range(1, bands)]
    along = [(lax.rem(lon + k, tiles), lat) for k in range(1, tiles)]
    barrier = pltpu.get_barrier_semaphore()
    for peer in beside + along:
        pl.semaphore_signal(
            barrier, inc=1, device_id=peer, device_id_type=pl.DeviceIdType.MESH
        )
    pl.semaphore_wait(barrier, len(beside) + len(along))

    def post(source, target, peer, number):
        copy = pltpu.make_async_remote_copy(
            src_ref=source,
            dst_ref=target,
            send_sem=send.at[number],
            recv_sem=recv.at[number],
            device_id=peer,
            device_id_type=pl.DeviceIdType.MESH,
        )
        copy.start()
        return copy

    copies = [post(x, held.at[lon, lat], peer, k) for k, peer in enumerate(beside)]
    own = pltpu.make_async_copy(x, held.at[lon, lat], own_sem)
    own.start()
    own.wait()
    for copy in copies:
        copy.wait()
    copies = [
        post(held.at[lon], held.at[lon], peer, len(beside) + k) for k, peer in enumerate(along)
    ]
    for copy in copies:
        copy.wait()
    if reduce:
        out[...] = jnp.sum(held[...], (0, 1))
    else:
        out[...] = held[...]


def gather(x, reduce, number):
    tiles = lax.axis_size("lon")
    bands = lax.axis_size("lat")
    full = (tiles, bands) + x.shape
    vmem = pl.BlockSpec(memory_space=pltpu.VMEM)
    peers = tiles + bands - 2
    return pl.pallas_call(
        functools.partial(gather_kernel, reduce, tiles, bands),
        out_shape=jax.ShapeDtypeStruct(x.shape if reduce else full, jnp.float32),
        in_specs=[vmem],
        out_specs=vmem,
        scratch_shapes=[
            pltpu.VMEM(full, jnp.float32),
            pltpu.SemaphoreType.DMA((peers,)),
            pltpu.SemaphoreType.DMA((peers,)),
            pltpu.SemaphoreType.DMA,
        ],
        cost_estimate=pl.CostEstimate(
            flops=0, bytes_accessed=20_000_000, transcendentals=0
        ),
        compiler_params=pltpu.CompilerParams(
            collective_id=number, has_side_effects=True, vmem_limit_bytes=24 * 1024 * 1024
        ),
        name=f"gather_{number}",
    )(x)


def local(
    kappa_east, kappa_north, depth, sigma, obs_precision, obs_tile, obs_col, obs_lat, innovation
):
    rows, lanes = kappa_east.shape
    total = sigma.shape[0]
    tiles = lax.axis_size("lon")
    bands = lax.axis_size("lat")
    devices = tiles * bands
    channels = -(-total // devices)
    listed = obs_col.shape[0]
    spare = channels * devices - total

    obs_lon = obs_tile[:, 0] * lanes + obs_col
    packed = jnp.concatenate(
        [
            kappa_east.reshape(-1),
            kappa_north.reshape(-1),
            depth.astype(jnp.float32).reshape(-1),
            obs_lon.astype(jnp.float32),
            obs_lat.astype(jnp.float32),
        ]
    ).reshape(-1, lanes)
    misfit = jnp.pad(obs_precision[:, None] * innovation, ((0, spare), (0, 0)))
    misfit = misfit.reshape(devices, channels, listed)
    misfit = lax.all_to_all(misfit, AXES, split_axis=0, concat_axis=0, tiled=True)
    packed = jnp.pad(packed, ((0, -packed.shape[0] % 8), (0, 0)))
    everywhere = gather(packed, False, 1)
    everywhere = everywhere.reshape((devices,) + packed.shape)
    used = 3 * rows + 2 * listed // lanes
    maps = everywhere[:, : 3 * rows].reshape(tiles, bands, 3, rows, lanes)
    maps = maps.transpose(2, 1, 3, 0, 4).reshape(3, bands * rows, tiles, lanes)
    places = everywhere[:, 3 * rows : used].reshape(tiles, bands, 2, listed)
    places = places.transpose(2, 1, 0, 3).reshape(2, bands, tiles * listed)
    misfit = misfit.reshape(tiles, bands, channels, listed).transpose(1, 2, 0, 3)
    misfit = misfit.reshape(bands, channels, tiles * listed)

    me = lax.axis_index("lon") * bands + lax.axis_index("lat")
    first = me * channels
    ids = first + jnp.arange(channels, dtype=jnp.int32)
    lev = jnp.where(ids < 2 * NZ, ids % NZ, 0).astype(jnp.float32)
    scale = lax.dynamic_slice(jnp.pad(sigma, (0, spare)), (first,), (channels,))
    weight = lax.dynamic_slice(jnp.pad(obs_precision, (0, spare)), (first,), (channels,))

    height = bands * rows
    ke, kn, deep = maps[0], maps[1], maps[2]

    def shifted(field, by):
        flat = field.reshape(height, tiles * lanes)
        return jnp.roll(flat, by, 1).reshape(field.shape)

    kept = (jnp.arange(height) < height - 1)[:, None, None]
    kn = jnp.where(kept, kn, 0.0)
    de = jnp.minimum(deep, shifted(deep, -1))
    faces = (
        ke,
        shifted(ke, 1),
        kn,
        de,
        shifted(de, 1),
        jnp.minimum(deep, jnp.roll(deep, -1, 0)),
    )

    values = jnp.concatenate([misfit, jnp.ones_like(misfit[:, :1])], axis=1)
    high = lax.reduce_precision(values, 8, 7)
    left = values - high
    middle = lax.reduce_precision(left, 8, 7)
    low = left - middle
    parts = jnp.stack([high, middle, low], axis=1).astype(jnp.bfloat16)
    at_row = places[1][:, None, :] == jnp.arange(rows, dtype=jnp.float32)[None, :, None]
    at_col = (
        places[0][:, None, :] == jnp.arange(tiles * lanes, dtype=jnp.float32)[None, :, None]
    )
    spread = jnp.where(at_row[:, None, None], parts[:, :, :, None, :], 0)
    spread = spread.reshape(bands, 3 * (channels + 1) * rows, tiles * listed)
    cells = lax.dot_general(
        spread,
        at_col.astype(jnp.bfloat16),
        (((2,), (2,)), ((0,), (0,))),
        preferred_element_type=jnp.float32,
    )
    cells = cells.reshape(bands, 3, channels + 1, rows, tiles, lanes).sum(1)
    cells = cells.transpose(1, 0, 2, 3, 4).reshape(channels + 1, height, tiles, lanes)
    wet = (deep[None] > lev[:, None, None, None]).astype(jnp.float32)
    scaled_wet = scale[:, None, None, None] * wet
    gain = scaled_wet * (scale * weight)[:, None, None, None] * cells[channels][None]

    def everyone(sums, number):
        partial = jnp.pad(jnp.sum(sums, 1), ((0, 8 - sums.shape[0]), (0, 0)))
        return jnp.sum(gather(partial, True, number), 1)

    def home(field):
        split = field.reshape(channels, bands, rows, tiles, lanes).transpose(3, 1, 0, 2, 4)
        split = split.reshape(devices, channels, rows, lanes)
        moved = lax.all_to_all(split, AXES, split_axis=0, concat_axis=0, tiled=True)
        return moved.reshape(devices * channels, rows, lanes)[:total]

    none = jnp.float32(0.0)
    (rhs,) = smooth("first", lev, none, faces, scaled_wet * cells[:channels])
    rhs_home = home(rhs)
    q_one, s_one, sums = smooth("curve", lev, none, faces, rhs, gain)
    sums = everyone(sums, 2)
    norm_zero, bend = sums[0], sums[1]
    alpha_one = norm_zero / (norm_zero + bend)
    r_one, t_one, sums = smooth("next", lev, alpha_one, faces, rhs, q_one, s_one, gain)
    sums, rhs_home = lax.optimization_barrier((sums, rhs_home))
    r_home = home(r_one)
    sums = everyone(sums, 3)
    norm_one = sums[0]
    beta = norm_one / norm_zero
    curve = (
        norm_one
        + sums[2]
        + 2.0 * beta * (sums[1] + sums[3])
        + beta * beta * (norm_zero + bend)
    )
    alpha_two = norm_one / curve
    (s_two,) = smooth("last", lev, beta, faces, q_one, t_one, gain)
    p_home = r_home + beta * rhs_home
    increment = alpha_one * rhs_home + alpha_two * p_home
    residual = r_home - alpha_two * (p_home + home(s_two))
    return increment, residual


def solution(mesh):
    return jax.shard_map(
        local,
        mesh=mesh,
        in_specs=(
            P("lat", "lon"),
            P("lat", "lon"),
            P("lat", "lon"),
            P(),
            P(),
            P(("lon", "lat"), None),
            P(("lon", "lat")),
            P(("lon", "lat")),
            P(None, ("lon", "lat")),
        ),
        out_specs=(P(None, "lat", "lon"), P(None, "lat", "lon")),
        check_vma=False,
    )
```

time: 220 us -> 209 us (0.950)
  Pallas kernels: 36.5 us -> 114 us
  waiting for transfers between devices: 84.5 us -> 28.7 us
  local copies, waits for them, and re-layouts: 35.5 us -> 19.5 us
  other arithmetic: 22.9 us -> 11.7 us
  starting transfers between devices: 32 us -> 23.7 us
  between operations: 3.86 us -> 7.43 us
    pallas_call x5 -> x7, Pallas kernels: 36.5 us -> 114 us  [the longest x3 74.3 us: gather(): pl.pallas_call(functools.partial(gather_kernel, reduce, tiles, bands), ou...]
    all_to_all x2 -> x3, waiting for transfers between devices: 61.3 us -> 28.7 us  [home(): moved = lax.all_to_all(split, AXES, split_axis=0, concat_axis=0, tiled=True)]
    all_to_all x4 -> x1, waiting for transfers between devices: 23.3 us -> 0.01 us  [local(): lax.all_to_all(misfit, AXES, split_axis=0, concat_axis=0, tiled=True)]
    all_to_all x4 -> x1, starting transfers between devices: 22.6 us -> 7.33 us  [local(): lax.all_to_all(misfit, AXES, split_axis=0, concat_axis=0, tiled=True)]
    unnamed x66 -> x24, local copies, waits for them, and re-layouts: 23.4 us -> 9.82 us
    reduce_sum x7 -> x4, other arithmetic: 10.7 us -> 0.27 us  [the longest x2 0.23 us: everyone(): return jnp.sum(gather(partial, True, number), 1)]
    all_to_all x2 -> x3, starting transfers between devices: 9.44 us -> 16.4 us  [home(): moved = lax.all_to_all(split, AXES, split_axis=0, concat_axis=0, tiled=True)]
    broadcast_in_dim x4 -> x0, local copies, waits for them, and re-layouts: 3.29 us -> none  [the longest x3 3.23 us: everyone(): jnp.broadcast_to(partial[None, ..., None], (devices,) + partial.shape + (...]
  transfers between devices with their start and end apart: 6 -> 4, of which waited for: 3 -> 1; matrix products, arithmetic and copies ran while one was open for 1% -> 6% of each run, Pallas kernels for 10% -> 51%
where the time goes in v3:
time: 209 us; the launch traced here: 208 us
  Pallas kernels  114 us (55%)
  waiting for transfers between devices  28.7 us (14%)
  starting transfers between devices  23.7 us (11%)
  local copies, waits for them, and re-layouts  19.5 us (9%)
  other arithmetic  11.7 us (6%)
  between operations  7.43 us (4%)
  matrix products  2.89 us (1%)
    pallas_call x3, Pallas kernels, gather(): pl.pallas_call(functools.partial(gather_kernel, reduce, tiles, bands), ou...  74.3 us
    pallas_call x4, Pallas kernels, smooth(): pl.pallas_call(functools.partial(smooth_kernel, stage), out_shape=shapes,...  40.1 us
    all_to_all x3, waiting for transfers between devices, home(): moved = lax.all_to_all(split, AXES, split_axis=0, concat_axis=0, tiled=True)  28.7 us
    all_to_all x3, starting transfers between devices, home(): moved = lax.all_to_all(split, AXES, split_axis=0, concat_axis=0, tiled=True)  16.4 us
    unnamed x24, local copies, waits for them, and re-layouts  9.82 us
    all_to_all x1, starting transfers between devices, local(): lax.all_to_all(misfit, AXES, split_axis=0, concat_axis=0, tiled=True)  7.33 us
  transfers between devices with their start and end apart: 4, of which 1 were waited for; matrix products, arithmetic and copies ran while one was open for 6% of the time, Pallas kernels for 51%

profile of v3, /device:TPU:0, one launch (start us, length us, event | category | flops | bytes accessed | tf_op | source)
XLA Modules:
  0.0 208.4 jit_solution(10388082442853973114)
XLA Ops:
  2.3 7.3 %all-to-all-start = ((f32[32,5,128]{2,1,0:T(8,128)}), f32[32,5,128]{2,1,0:T(8,128)S(1)}, u32[]{:S(2)}, u32[]{:S(2)}) async-start(f32[32,5,128]{2,1,0:T(8,128)} %reshape.171), calls=%async_computation | async-start | bytes 262144 | tf_op jit(solution)/shard_map/all_to_all | solution.py:255
  13.1 23.5 %gather_1.1 = f32[8,4,56,128]{3,2,1,0:T(8,128)S(1)} custom-call(f32[56,128]{1,0:T(8,128)S(1)} %pad.24.x), custom_call_target="tpu_custom_call" | custom-call | bytes 20000000 | tf_op jit(solution)/shard_map/gather_1/pallas_call | solution.py:210
  39.5 2.9 %fusion = f32[4,288,1024]{2,1,0:T(8,128)S(1)} fusion(bf16[4,288,1024]{2,1,0:T(8,128)(2,1)S(1)} %bitcast.128, f32[4,1024]{1,0:T(4,128)S(1)} %bitcast.140), kind=kOutput, calls=%fused_computation.1 | convolution fusion | flops 2420113408 | bytes 7094272 | tf_op jit(solution)/shard_map/dot_general | solution.py:305
  42.4 3.3 %copy.48 = f32[144,8,8,128]{3,2,1,0:T(8,128)} copy(f32[144,8,8,128]{3,1,2,0:T(8,128)S(1)} %bitcast.126) | data formatting | bytes 9437184
  45.7 2.9 %reduce_sum.45 = f32[4,6,16,8,128]{4,3,2,1,0:T(8,128)S(1)} reduce(f32[4,3,6,16,8,128]{5,4,3,2,1,0:T(8,128)} %bitcast.115, f32[]{:T(128)} %constant.40.clone.1), dimensions={1}, to_apply=%region_0.1 | reduce | flops 786432 | bytes 6291460 | tf_op jit(solution)/shard_map/reduce_sum | solution.py:311
  48.9 1.4 fusion.2
  50.3 7.3 %smooth_first.1.rest_0_ = f32[5,64,8,128]{3,2,1,0:T(8,128)S(1)} custom-call(f32[5]{0:T(128)S(1)} %fusion.13.lev, f32[1]{0:T(128)} %constant.38.clone.1.scalar, f32[64,8,128]{2,1,0:T(8,128)S(1)} %bitcast.99, f32[64,8,128]{2,1,0:T(8,128)S(1)} %bitcast.107, f32[64,8,128]{2,1,0:T(8,128)S(1)} %get-tuple-element.42.kn, f32[64,8,128]{2,1,0:T(8,128)S(1)} %get-tuple-element.28.de, ...), custom_call_target="tpu_custom_call" | custom-call | flops 19660800 | bytes 5242880 | tf_op jit(solution)/shard_map/smooth_first/pallas_call | solution.py:150
  57.6 1.3 copy.40
  58.9 9.8 %all-to-all-start.1 = ((f32[32,5,16,128]{3,2,1,0:T(8,128)}), f32[32,5,16,128]{3,2,1,0:T(8,128)}, u32[]{:S(2)}, u32[]{:S(2)}) async-start(f32[32,5,16,128]{3,2,1,0:T(8,128)} %bitcast.123), calls=%async_computation.1 | async-start | bytes 2621440 | tf_op jit(solution)/shard_map/all_to_all | solution.py:324
  68.7 14.6 %smooth_curve.1 = (f32[5,64,8,128]{3,2,1,0:T(8,128)S(1)}, f32[5,64,8,128]{3,2,1,0:T(8,128)S(1)}, f32[2,8,128]{2,1,0:T(8,128)S(1)}) custom-call(f32[5]{0:T(128)S(1)} %fusion.13.lev, f32[1]{0:T(128)} %constant.38.clone.1.scalar, f32[64,8,128]{2,1,0:T(8,128)S(1)} %bitcast.100, f32[64,8,128]{2,1,0:T(8,128)S(1)} %bitcast.108, ...), custom_call_target="tpu_custom_call" | custom-call | flops 39321600 | bytes 5242880 | tf_op jit(solution)/shard_map/smooth_curve/pallas_call | solution.py:150
  83.4 1.1 copy-done
  85.5 18.2 %gather_2.1 = f32[8,128]{1,0:T(8,128)S(1)} custom-call(f32[8,128]{1,0:T(8,128)S(1)} %pad.28.x), custom_call_target="tpu_custom_call" | custom-call | bytes 20000000 | tf_op jit(solution)/shard_map/gather_2/pallas_call | solution.py:210
  106.3 9.8 %smooth_next.1 = (f32[5,64,8,128]{3,2,1,0:T(8,128)S(1)}, f32[5,64,8,128]{3,2,1,0:T(8,128)S(1)}, f32[4,8,128]{2,1,0:T(8,128)S(1)}) custom-call(f32[5]{0:T(128)S(1)} %fusion.13.lev, f32[1]{0:T(128)} %bitcast.28.scalar, f32[64,8,128]{2,1,0:T(8,128)S(1)} %bitcast.101, f32[64,8,128]{2,1,0:T(8,128)S(1)} %bitcast.109, f32[64,8,128]{2,1,0:T(8,128)S(1)} %get-tuple-element.42.kn, ...), custom_call_target="tpu_custom_call" | custom-call | flops 19660800 | bytes 5242880 | tf_op jit(solution)/shard_map/smooth_next/pallas_call | solution.py:150
  116.1 1.1 copy-done.2
  117.2 1.3 copy.41
  118.5 3.4 %all-to-all-start.2 = ((f32[32,5,16,128]{3,2,1,0:T(8,128)}), f32[32,5,16,128]{3,2,1,0:T(8,128)}, u32[]{:S(2)}, u32[]{:S(2)}) async-start(f32[32,5,16,128]{3,2,1,0:T(8,128)} %bitcast.38), calls=%async_computation.2 | async-start | bytes 2621440 | tf_op jit(solution)/shard_map/all_to_all | solution.py:324
  121.9 2.5 %slice.137 = f32[151,16,128]{2,1,0:T(8,128)} slice(f32[160,16,128]{2,1,0:T(8,128)} %bitcast.32), slice={[0:151], [0:16], [0:128]} | slice | bytes 2473984 | tf_op jit(solution)/shard_map/slice | solution.py:325
  124.5 32.6 %gather_3.1 = f32[8,128]{1,0:T(8,128)S(1)} custom-call(f32[8,128]{1,0:T(8,128)S(1)} %pad.29.x), custom_call_target="tpu_custom_call" | custom-call | bytes 20000000 | tf_op jit(solution)/shard_map/gather_3/pallas_call | solution.py:210
  159.2 1.3 copy-done.3
  160.5 8.4 %smooth_last.1 = f32[5,64,8,128]{3,2,1,0:T(8,128)S(1)} custom-call(f32[5]{0:T(128)S(1)} %fusion.13.lev, f32[1]{0:T(128)} %bitcast.40.scalar, f32[64,8,128]{2,1,0:T(8,128)S(1)} %bitcast.102, f32[64,8,128]{2,1,0:T(8,128)S(1)} %bitcast.110, f32[64,8,128]{2,1,0:T(8,128)S(1)} %get-tuple-element.42.kn, f32[64,8,128]{2,1,0:T(8,128)S(1)} %get-tuple-element.28.de, ...), custom_call_target="tpu_custom_call" | custom-call | flops 19660800 | bytes 5242880 | tf_op jit(solution)/shard_map/smooth_last/pallas_call | solution.py:150
  168.9 1.3 copy.42
  170.2 3.2 %all-to-all-start.3 = ((f32[32,5,16,128]{3,2,1,0:T(8,128)}), f32[32,5,16,128]{3,2,1,0:T(8,128)S(1)}, u32[]{:S(2)}, u32[]{:S(2)}) async-start(f32[32,5,16,128]{3,2,1,0:T(8,128)} %bitcast.43), calls=%async_computation.3 | async-start | bytes 2621440 | tf_op jit(solution)/shard_map/all_to_all | solution.py:324
  176.6 28.7 %all-to-all-done.3 = f32[32,5,16,128]{3,2,1,0:T(8,128)S(1)} async-done(((f32[32,5,16,128]{3,2,1,0:T(8,128)}), f32[32,5,16,128]{3,2,1,0:T(8,128)S(1)}, u32[]{:S(2)}, u32[]{:S(2)}) %all-to-all-start.3) | async-done | bytes 1310752 | tf_op jit(solution)/shard_map/all_to_all | solution.py:324
  205.3 3.1 %fusion.4 = (f32[151,16,128]{2,1,0:T(8,128)}, f32[151,16,128]{2,1,0:T(8,128)}) fusion(f32[160,16,128]{2,1,0:T(8,128)S(1)} %bitcast.125, f32[160,16,128]{2,1,0:T(8,128)} %bitcast.39, f32[151,16,128]{2,1,0:T(8,128)S(1)} %copy-done.5, f32[]{:T(128)} %div.10, f32[]{:T(128)S(6)} %div.11, f32[]{:T(128)} %div.9), kind=kLoop, calls=%fused_computation.9 | loop fusion | flops 2473984 | bytes 6184972 | tf_op jit(solution)/shard_map/sub | solution.py:350
  (68 shorter events, 10.6 us)
Async XLA Ops:
  2.3 36.7 %all-to-all-start = ((f32[32,5,128]{2,1,0:T(8,128)}), f32[32,5,128]{2,1,0:T(8,128)S(1)}, u32[]{:S(2)}, u32[]{:S(2)}) async-start(f32[32,5,128]{2,1,0:T(8,128)} %reshape.171), calls=%async_computation | async-start | bytes 262144 | tf_op jit(solution)/shard_map/all_to_all | solution.py:255
  38.2 0.7 copy-start.6
  38.2 0.7 copy-start.7
  58.9 59.6 %all-to-all-start.1 = ((f32[32,5,16,128]{3,2,1,0:T(8,128)}), f32[32,5,16,128]{3,2,1,0:T(8,128)}, u32[]{:S(2)}, u32[]{:S(2)}) async-start(f32[32,5,16,128]{3,2,1,0:T(8,128)} %bitcast.123), calls=%async_computation.1 | async-start | bytes 2621440 | tf_op jit(solution)/shard_map/all_to_all | solution.py:324
  83.4 1.1 copy-start
  84.4 1.0 copy-start.4
  116.1 1.1 copy-start.2
  118.5 51.7 %all-to-all-start.2 = ((f32[32,5,16,128]{3,2,1,0:T(8,128)}), f32[32,5,16,128]{3,2,1,0:T(8,128)}, u32[]{:S(2)}, u32[]{:S(2)}) async-start(f32[32,5,16,128]{3,2,1,0:T(8,128)} %bitcast.38), calls=%async_computation.2 | async-start | bytes 2621440 | tf_op jit(solution)/shard_map/all_to_all | solution.py:324
  121.9 37.2 %copy-start.1 = (f32[5,64,8,128]{3,2,1,0:T(8,128)S(1)}, f32[5,64,8,128]{3,2,1,0:T(8,128)}, u32[]{:S(2)}) copy-start(f32[5,64,8,128]{3,2,1,0:T(8,128)} %copy-done) | copy-start | bytes 3932164
  159.2 1.3 copy-start.3
  170.2 35.1 %copy-start.5 = (f32[151,16,128]{2,1,0:T(8,128)S(1)}, f32[151,16,128]{2,1,0:T(8,128)}, u32[]{:S(2)}) copy-start(f32[151,16,128]{2,1,0:T(8,128)} %slice.137) | copy-start | bytes 3710980
  170.2 35.1 %all-to-all-start.3 = ((f32[32,5,16,128]{3,2,1,0:T(8,128)}), f32[32,5,16,128]{3,2,1,0:T(8,128)S(1)}, u32[]{:S(2)}, u32[]{:S(2)}) async-start(f32[32,5,16,128]{3,2,1,0:T(8,128)} %bitcast.43), calls=%async_computation.3 | async-start | bytes 2621440 | tf_op jit(solution)/shard_map/all_to_all | solution.py:324
